TPU v7x, 256 devices: a whole 4x4x8 slice. The times are simulated.
256 devices in a mesh: seq: 32 (over y, z), head: 8 (over x, core).
Axes of the slice: x: 4, y: 4, z: 8, core: 2. Of those that a mesh axis runs over, the one named last changes fastest.
Arguments:
- inputs: bfloat16 [8192, 8192], P('seq'), may hold values from -6 to 6
- w_value: bfloat16 [8192, 4096], P('seq', 'head'), may hold values from -0.0625 to 0.0625
- log_decay: float32 [8192, 64], P('seq', 'head'), may hold values from -1 to 0
- b_proj: bfloat16 [8192, 128], P('seq'), may hold values from -0.5 to 0.5
- c_proj: bfloat16 [8192, 128], P('seq'), may hold values from -0.5 to 0.5
- grad_out: bfloat16 [8192, 4096], P('seq', 'head'), may hold values from -6 to 6
Outputs:
- grad_input: bfloat16 [8192, 8192], P('seq', 'head')
- grad_weight: float32 [8192, 4096], P('seq', 'head')
- grad_b: float32 [8192, 128], P('seq')
- grad_c: float32 [8192, 128], P('seq')
All inputs are finite; a program needn't handle non-finite values.
Results may differ from a plain program's by a relative error of at most 0.027.
Values may be sent and summed in bfloat16 or wider, within the bound.
A program may use at most 128 MiB of HBM per device.

v0:
```python
import jax
import jax.numpy as jnp
from jax import lax
from jax.sharding import PartitionSpec as P

SPAN = 256


HIGH = lax.Precision.HIGHEST


def carried_in(array, axis, combine, identity, reverse):
    length, index = (lax.axis_size(axis), lax.axis_index(axis))
    everything = jax.tree.map(
        lambda part, kind: lax.all_gather(part.astype(kind), axis),
        array,
        (jnp.bfloat16, jnp.bfloat16),
    )
    start = jax.tree.map(
        lambda part, zero: jnp.broadcast_to(jnp.asarray(zero, part.dtype), part.shape),
        array,
        identity,
    )

    def lap(k, before):
        at = length - 1 - k if reverse else k
        reached = at > index if reverse else at < index
        new = combine(
            before, jax.tree.map(lambda part, own: part[at].astype(own.dtype), everything, array)
        )
        return jax.tree.map(lambda a, b: jnp.where(reached, a, b), new, before)

    return lax.fori_loop(0, length, lap, start)


def link(earlier, later):
    return (earlier[0] * later[0], later[0][:, None, None] * earlier[1] + later[1])


def advance_once(carried, item):
    decay, local = item
    return (decay[:, None, None] * carried + local, carried)


def per_device(inputs, w_value, log_decay, b_proj, c_proj, grad_out):
    steps = inputs.shape[0]
    heads = log_decay.shape[1]
    columns = grad_out.shape[1]
    depth = columns // heads
    states = b_proj.shape[1]
    blocks = steps // SPAN
    w_full = lax.all_gather(w_value, "seq", axis=0, tiled=True)
    values = jnp.dot(inputs, w_full, preferred_element_type=jnp.float32).astype(jnp.bfloat16)
    xs = values.astype(jnp.float32).reshape(blocks, SPAN, heads, depth)
    dys = grad_out.astype(jnp.float32).reshape(blocks, SPAN, heads, depth)
    bs = b_proj.astype(jnp.float32).reshape(blocks, SPAN, states)
    cs = c_proj.astype(jnp.float32).reshape(blocks, SPAN, states)
    cum_log = jnp.cumsum(log_decay.reshape(blocks, SPAN, heads), axis=1)
    totals = cum_log[:, -1]
    grow = jnp.exp(cum_log)
    shrink = jnp.exp(totals[:, None] - cum_log)
    cum_heads = jnp.swapaxes(cum_log, 1, 2)
    rows = lax.broadcasted_iota(jnp.int32, (SPAN, SPAN), 0)
    cols = lax.broadcasted_iota(jnp.int32, (SPAN, SPAN), 1)
    lower = (rows >= cols)[None, None]
    diff = cum_heads[:, :, :, None] - cum_heads[:, :, None, :]
    decay_mat = jnp.exp(jnp.where(lower, diff, -jnp.inf))
    cross = jnp.einsum("kthp,kjhp->khtj", dys, xs, precision=HIGH)
    mixed = decay_mat * cross
    scores = jnp.einsum("ktn,kjn->ktj", cs, bs, precision=HIGH)
    span_decay = jnp.exp(totals)
    dev_decay = jnp.exp(jnp.sum(totals, axis=0))
    zero_state = jnp.zeros((heads, depth, states), jnp.float32)
    identity_matrix = (jnp.ones_like(dev_decay), zero_state)
    local_end = jnp.einsum("kjhp,kjh,kjn->khpn", xs, shrink, bs, precision=HIGH)
    dev_state, before = lax.scan(advance_once, zero_state, (span_decay, local_end))
    incoming = carried_in((dev_decay, dev_state), "seq", link, identity_matrix, False)[1]
    lead = jnp.exp(jnp.cumsum(totals, axis=0) - totals)
    state_in = before + lead[:, :, None, None] * incoming[None]
    grad_c = jnp.einsum("kthp,khpn,kth->ktn", dys, state_in, grow, precision=HIGH)
    grad_c = grad_c + jnp.einsum("khtj,kjn->ktn", mixed, bs, precision=HIGH)
    local_back = jnp.einsum("kthp,kth,ktn->khpn", dys, grow, cs, precision=HIGH)
    dev_back, after = lax.scan(advance_once, zero_state, (span_decay, local_back), reverse=True)
    incoming_back = carried_in((dev_decay, dev_back), "seq", link, identity_matrix, True)[1]
    trail = jnp.exp(jnp.sum(totals, axis=0)[None] - jnp.cumsum(totals, axis=0))
    grad_in = after + trail[:, :, None, None] * incoming_back[None]
    grad_vals = jnp.einsum("khst,kst,kshp->kthp", decay_mat, scores, dys, precision=HIGH)
    grad_vals = grad_vals + jnp.einsum("khpn,ktn,kth->kthp", grad_in, bs, shrink, precision=HIGH)
    grad_b = jnp.einsum("khst,ksn->ktn", mixed, cs, precision=HIGH)
    grad_b = grad_b + jnp.einsum("kthp,khpn,kth->ktn", xs, grad_in, shrink, precision=HIGH)
    grad_values = grad_vals.reshape(steps, columns).astype(jnp.bfloat16)
    grad_b, grad_c = (
        lax.psum(grad_b.reshape(steps, states).astype(jnp.bfloat16), "head").astype(jnp.float32),
        lax.psum(grad_c.reshape(steps, states).astype(jnp.bfloat16), "head").astype(jnp.float32),
    )
    term = lax.dot_general(
        grad_values, w_full, (((1,), (1,)), ((), ())), preferred_element_type=jnp.float32
    )
    grad_input = lax.psum_scatter(
        term.astype(jnp.bfloat16), "head", scatter_dimension=1, tiled=True
    )
    grad_weight = lax.psum_scatter(
        lax.dot_general(
            inputs, grad_values, (((0,), (0,)), ((), ())), preferred_element_type=jnp.float32
        ).astype(jnp.bfloat16),
        "seq",
        scatter_dimension=0,
        tiled=True,
    ).astype(jnp.float32)
    return (grad_input, grad_weight, grad_b, grad_c)


def solution(mesh):
    placed = (
        P("seq", None),
        P("seq", "head"),
        P("seq", "head"),
        P("seq", None),
        P("seq", None),
        P("seq", "head"),
    )
    return jax.shard_map(
        per_device,
        mesh=mesh,
        in_specs=placed,
        out_specs=(P("seq", "head"), P("seq", "head"), P("seq", None), P("seq", None)),
        check_vma=False,
    )
```

profile of v0, /device:TPU:1, one launch (start us, length us, event | category | flops | bytes accessed | tf_op | source)
XLA Modules:
  0.0 653.8 jit_solution(10136107935495648219)
XLA Ops:
  8.0 1.3 reduce-window.6
  9.4 1.1 copy.32
  10.8 1.9 fusion.18
  13.0 37.4 %all-gather = bf16[32,1,8]{2,1,0:T(2,128)(2,1)S(1)} all-gather(bf16[1,1,8]{2,1,0:T(2,128)(2,1)S(1)} %copy.34), channel_id=2, replica_groups=mesh['seq'=32,'head'=8] {'seq'}, dimensions={0}, use_global_device_ids=true | all-gather | bytes 528 | tf_op jit(solution)/shard_map/all_gather | solution.py:15
  50.5 1.0 fusion.43
  51.6 60.7 %all-gather.7.cloned.1.call-done = bf16[8192,512]{1,0:T(8,128)(2,1)} async-done(((bf16[256,512]{1,0:T(8,128)(2,1)}), bf16[8192,512]{1,0:T(8,128)(2,1)}) %all-gather.7.cloned.1.call-update) | async-done | bytes 8388624 | tf_op jit(solution)/shard_map/all_gather | solution.py:52
  112.2 7.0 %convolution_convert_fusion.2 = bf16[256,512]{1,0:T(8,128)(2,1)S(1)} fusion(bf16[256,8192]{1,0:T(8,128)(2,1)} %param.10, bf16[8192,512]{1,0:T(8,128)(2,1)} %all-gather.7.cloned.1.call-done), kind=kOutput, calls=%fused_computation.21 | convolution fusion | flops 2147614720 | bytes 12845056 | tf_op jit(solution)/shard_map/dot_general | solution.py:53
  119.4 1.1 fusion.19
  120.5 71.6 %all-gather.9.cloned.1.call-done = bf16[256,64,128]{2,1,0:T(8,128)(2,1)} async-done(((bf16[8,64,128]{2,1,0:T(8,128)(2,1)}), bf16[256,64,128]{2,1,0:T(8,128)(2,1)}) %all-gather.9.cloned.1.call-update) | async-done | bytes 4194320 | tf_op jit(solution)/shard_map/all_gather | solution.py:15
  192.1 34.1 %while.40 = (s32[]{:T(128)}, f32[8,64,128]{2,1,0:T(8,128)S(1)}, s32[]{:T(128)}, bf16[32,8]{1,0:T(8,128)(2,1)S(1)}, bf16[32,8,64,128]{3,2,1,0:T(8,128)(2,1)}, /*index=5*/s32[]{:T(128)}, s32[]{:T(128)}, s32[]{:T(128)}, s32[]{:T(128)}) while((s32[]{:T(128)}, f32[8,64,128]{2,1,0:T(8,128)S(1)}, s32[]{:T(128)}, ...), condition=%wide.region_3.4_spmd.clone, body=%wide.region_2.3_spmd.clone.sunk | while | flops 327696 | bytes 655607 | solution.py:33
  193.1 1.0 fusion.61
  194.2 1.0 fusion.61
  207.0 1.0 fusion.61
  208.1 1.0 fusion.61
  216.6 1.0 fusion.61
  222.0 1.0 fusion.61
  224.1 1.0 fusion.61
  225.2 1.0 fusion.61
  226.6 1.6 fusion.15
  228.3 1.0 convolution_bitcast_fusion.2
  231.0 43.4 %all-gather.11.cloned.1.call-done = bf16[256,64,128]{2,1,0:T(8,128)(2,1)} async-done(((bf16[8,64,128]{2,1,0:T(8,128)(2,1)}), bf16[256,64,128]{2,1,0:T(8,128)(2,1)}) %all-gather.11.cloned.1.call-update) | async-done | bytes 4194320 | tf_op jit(solution)/shard_map/all_gather | solution.py:15
  274.3 33.7 %while.41 = (s32[]{:T(128)}, f32[8,64,128]{2,1,0:T(8,128)S(1)}, s32[]{:T(128)}, bf16[32,8]{1,0:T(8,128)(2,1)S(1)}, bf16[32,8,64,128]{3,2,1,0:T(8,128)(2,1)}, /*index=5*/s32[]{:T(128)}, s32[]{:T(128)}) while((s32[]{:T(128)}, f32[8,64,128]{2,1,0:T(8,128)S(1)}, s32[]{:T(128)}, bf16[32,8]{1,0:T(8,128)(2,1)S(1)}, ...), condition=%wide.region_9.10_spmd.clone, body=%wide.region_8.9_spmd.clone.sunk | while | flops 327692 | bytes 655545 | solution.py:33
  308.0 1.0 convolution_bitcast_fusion.1
  309.1 1.0 fusion.21
  310.1 7.8 %fusion.2 = bf16[8192,512]{0,1:T(8,128)(2,1)} fusion(bf16[256,512]{0,1:T(8,128)(2,1)S(1)} %bitcast.122, bf16[256,8192]{1,0:T(8,128)(2,1)} %param.10), kind=kOutput, calls=%fused_computation.7 | convolution fusion | flops 2151677952 | bytes 12845056 | tf_op jit(solution)/shard_map/dot_general | solution.py:103
  318.2 7.7 %convolution_convert_fusion.1 = bf16[256,8192]{1,0:T(8,128)(2,1)} fusion(bf16[256,512]{0,1:T(8,128)(2,1)S(1)} %bitcast.123, bf16[8192,512]{1,0:T(8,128)(2,1)} %all-gather.7.cloned.1.call-done), kind=kOutput, calls=%fused_computation.8 | convolution fusion | flops 2149580800 | bytes 12845056 | tf_op jit(solution)/shard_map/dot_general | solution.py:96
  325.9 46.5 %all-reduce.3.cloned.1.call-done = (bf16[256,128]{1,0:T(8,128)(2,1)}, bf16[256,128]{1,0:T(8,128)(2,1)}) async-done(((bf16[256,128]{1,0:T(8,128)(2,1)}, bf16[256,128]{1,0:T(8,128)(2,1)}), (bf16[256,128]{1,0:T(8,128)(2,1)}, bf16[256,128]{1,0:T(8,128)(2,1)})) %all-reduce.3.cloned.1.call-update) | async-done | bytes 131088 | tf_op jit(solution)/shard_map/psum | solution.py:93
  372.5 1.5 convert_element_type.131
  374.0 1.5 convert_element_type.135
  375.5 228.6 %reduce-scatter.5.cloned.1.call-done = bf16[256,512]{0,1:T(8,128)(2,1)} async-done(((bf16[8192,512]{0,1:T(8,128)(2,1)}), bf16[256,512]{0,1:T(8,128)(2,1)}) %reduce-scatter.5.cloned.1.call-update) | async-done | bytes 262160 | tf_op jit(solution)/shard_map/reduce_scatter | solution.py:102
  604.1 1.9 copy.39
  606.0 41.0 %reduce-scatter.3.cloned.1.call-done = bf16[256,1024]{1,0:T(8,128)(2,1)} async-done(((bf16[256,8192]{1,0:T(8,128)(2,1)}), bf16[256,1024]{1,0:T(8,128)(2,1)}) %reduce-scatter.3.cloned.1.call-update) | async-done | bytes 524304 | tf_op jit(solution)/shard_map/reduce_scatter | solution.py:99
  (154 shorter events, 61.6 us)
Async XLA Ops:
  7.2 43.4 %copy-start = (bf16[256,128]{1,0:T(8,128)(2,1)S(1)}, bf16[256,128]{1,0:T(8,128)(2,1)}, u32[]{:S(2)}) copy-start(bf16[256,128]{1,0:T(8,128)(2,1)} %param.13) | copy-start | bytes 196612
  7.2 105.1 %all-gather.7.cloned.1.call-start = ((), (), s32[]{:S(2)}) async-start(), calls=%async_computation.2 | async-start | bytes 8650752 | tf_op jit(solution)/shard_map/all_gather | solution.py:52
  7.9 184.2 %all-gather.9.cloned.1.call-start = ((), (), s32[]{:S(2)}) async-start(), calls=%async_computation.5 | async-start | bytes 4325376 | tf_op jit(solution)/shard_map/all_gather | solution.py:15
  12.7 261.6 %all-gather.11.cloned.1.call-start = ((), (), s32[]{:S(2)}) async-start(), calls=%async_computation.6 | async-start | bytes 4325376 | tf_op jit(solution)/shard_map/all_gather | solution.py:15
  120.5 252.0 %all-reduce.3.cloned.1.call-start = ((), (), s32[]{:S(2)}) async-start(), calls=%async_computation.7 | async-start | bytes 262144 | tf_op jit(solution)/shard_map/psum | solution.py:93
  226.2 3.8 copy-start.1
  310.1 294.0 %reduce-scatter.5.cloned.1.call-start = ((), (), s32[]{:S(2)}) async-start(), calls=%async_computation.4 | async-start | bytes 8650752 | tf_op jit(solution)/shard_map/reduce_scatter | solution.py:102
  317.9 329.1 %reduce-scatter.3.cloned.1.call-start = ((), (), s32[]{:S(2)}) async-start(), calls=%async_computation.3 | async-start | bytes 4718592 | tf_op jit(solution)/shard_map/reduce_scatter | solution.py:99
Sparse Core Ops, SparseCore 0:
  10.6 101.5 all-gather.6
  115.4 76.6 all-gather.8
  195.2 79.0 all-gather.10
  310.2 62.1 all-reduce.2
  376.9 227.1 reduce-scatter.4
  607.1 39.8 reduce-scatter.2
where the time goes:
time: 657 us; the launch traced here: 654 us
  waiting for transfers between devices  493 us (75%)
  other arithmetic  70.2 us (11%)
  blocking collectives  37.4 us (6%)
  matrix products  33.2 us (5%)
  between operations  14.2 us (2%)
    reduce_scatter x1, waiting for transfers between devices, per_device(): lax.psum_scatter(lax.dot_general(inputs, grad_values, (((0,), (0,)), ((),...  229 us
    all_gather x2, waiting for transfers between devices, carried_in(): lax.all_gather(part.astype(kind), axis)  115 us
    select_n x64, other arithmetic, lap(): return jax.tree.map(lambda a, b: jnp.where(reached, a, b), new, before)  64.9 us
    all_gather x1, waiting for transfers between devices, per_device(): w_full = lax.all_gather(w_value, 'seq', axis=0, tiled=True)  60.7 us
    psum x1, waiting for transfers between devices, per_device(): lax.psum(grad_b.reshape(steps, states).astype(jnp.bfloat16), 'head')  46.5 us
    reduce_scatter x1, waiting for transfers between devices, per_device(): lax.psum_scatter(term.astype(jnp.bfloat16), 'head', scatter_dimension=1,...  41 us
    all_gather x1, blocking collectives, carried_in(): lax.all_gather(part.astype(kind), axis)  37.4 us
  transfers between devices with their start and end apart: 6, of which 6 were waited for; matrix products, arithmetic and copies ran while one was open for 11% of the time, Pallas kernels for 0%

commit v1 on v0

--- a/solution.py
+++ b/solution.py
@@ -55,7 +55,10 @@
     dys = grad_out.astype(jnp.float32).reshape(blocks, SPAN, heads, depth)
     bs = b_proj.astype(jnp.float32).reshape(blocks, SPAN, states)
     cs = c_proj.astype(jnp.float32).reshape(blocks, SPAN, states)
-    cum_log = jnp.cumsum(log_decay.reshape(blocks, SPAN, heads), axis=1)
+    before_or_at = jnp.tril(jnp.ones((SPAN, SPAN), jnp.float32))
+    cum_log = jnp.einsum(
+        "tj,kjh->kth", before_or_at, log_decay.reshape(blocks, SPAN, heads), precision=HIGH
+    )
     totals = cum_log[:, -1]
     grow = jnp.exp(cum_log)
     shrink = jnp.exp(totals[:, None] - cum_log)
@@ -75,14 +78,16 @@
     local_end = jnp.einsum("kjhp,kjh,kjn->khpn", xs, shrink, bs, precision=HIGH)
     dev_state, before = lax.scan(advance_once, zero_state, (span_decay, local_end))
     incoming = carried_in((dev_decay, dev_state), "seq", link, identity_matrix, False)[1]
-    lead = jnp.exp(jnp.cumsum(totals, axis=0) - totals)
+    earlier = jnp.tril(jnp.ones((blocks, blocks), jnp.float32))
+    through = jnp.einsum("kl,lh->kh", earlier, totals, precision=HIGH)
+    lead = jnp.exp(through - totals)
     state_in = before + lead[:, :, None, None] * incoming[None]
     grad_c = jnp.einsum("kthp,khpn,kth->ktn", dys, state_in, grow, precision=HIGH)
     grad_c = grad_c + jnp.einsum("khtj,kjn->ktn", mixed, bs, precision=HIGH)
     local_back = jnp.einsum("kthp,kth,ktn->khpn", dys, grow, cs, precision=HIGH)
     dev_back, after = lax.scan(advance_once, zero_state, (span_decay, local_back), reverse=True)
     incoming_back = carried_in((dev_decay, dev_back), "seq", link, identity_matrix, True)[1]
-    trail = jnp.exp(jnp.sum(totals, axis=0)[None] - jnp.cumsum(totals, axis=0))
+    trail = jnp.exp(jnp.sum(totals, axis=0)[None] - through)
     grad_in = after + trail[:, :, None, None] * incoming_back[None]
     grad_vals = jnp.einsum("khst,kst,kshp->kthp", decay_mat, scores, dys, precision=HIGH)
     grad_vals = grad_vals + jnp.einsum("khpn,ktn,kth->kthp", grad_in, bs, shrink, precision=HIGH)

time: 657 us -> 658 us (level)
  no operation moved by 1% of the time
where the time goes in v1:
time: 658 us; the launch traced here: 654 us
  waiting for transfers between devices  494 us (75%)
  other arithmetic  68.8 us (10%)
  blocking collectives  36.9 us (6%)
  matrix products  34.2 us (5%)
  between operations  14.2 us (2%)
    reduce_scatter x1, waiting for transfers between devices, per_device(): lax.psum_scatter(lax.dot_general(inputs, grad_values, (((0,), (0,)), ((),...  229 us
    all_gather x2, waiting for transfers between devices, carried_in(): lax.all_gather(part.astype(kind), axis)  115 us
    select_n x64, other arithmetic, lap(): return jax.tree.map(lambda a, b: jnp.where(reached, a, b), new, before)  65 us
    all_gather x1, waiting for transfers between devices, per_device(): w_full = lax.all_gather(w_value, 'seq', axis=0, tiled=True)  62.1 us
    psum x1, waiting for transfers between devices, per_device(): lax.psum(grad_b.reshape(steps, states).astype(jnp.bfloat16), 'head')  46.5 us
    reduce_scatter x1, waiting for transfers between devices, per_device(): lax.psum_scatter(term.astype(jnp.bfloat16), 'head', scatter_dimension=1,...  41 us
    all_gather x1, blocking collectives, carried_in(): lax.all_gather(part.astype(kind), axis)  36.9 us
  transfers between devices with their start and end apart: 6, of which 6 were waited for; matrix products, arithmetic and copies ran while one was open for 11% of the time, Pallas kernels for 0%

profile of v1, /device:TPU:1, one launch (start us, length us, event | category | flops | bytes accessed | tf_op | source)
XLA Modules:
  0.0 654.2 jit_solution(16976083974051187872)
XLA Ops:
  8.0 1.1 copy.24
  10.2 1.9 fusion.18
  12.4 36.9 %all-gather = bf16[32,1,8]{2,1,0:T(2,128)(2,1)S(1)} all-gather(bf16[1,1,8]{2,1,0:T(2,128)(2,1)S(1)} %copy.26), channel_id=2, replica_groups=mesh['seq'=32,'head'=8] {'seq'}, dimensions={0}, use_global_device_ids=true | all-gather | bytes 528 | tf_op jit(solution)/shard_map/all_gather | solution.py:15
  49.4 1.0 fusion.47
  50.4 62.1 %all-gather.7.cloned.1.call-done = bf16[8192,512]{1,0:T(8,128)(2,1)} async-done(((bf16[256,512]{1,0:T(8,128)(2,1)}), bf16[8192,512]{1,0:T(8,128)(2,1)}) %all-gather.7.cloned.1.call-update) | async-done | bytes 8388624 | tf_op jit(solution)/shard_map/all_gather | solution.py:52
  112.5 7.0 %convolution_convert_fusion.2 = bf16[256,512]{1,0:T(8,128)(2,1)S(1)} fusion(bf16[256,8192]{1,0:T(8,128)(2,1)} %param.10, bf16[8192,512]{1,0:T(8,128)(2,1)} %all-gather.7.cloned.1.call-done), kind=kOutput, calls=%fused_computation.21 | convolution fusion | flops 2147614720 | bytes 12845056 | tf_op jit(solution)/shard_map/dot_general | solution.py:53
  119.7 1.1 fusion.19
  120.8 71.6 %all-gather.9.cloned.1.call-done = bf16[256,64,128]{2,1,0:T(8,128)(2,1)} async-done(((bf16[8,64,128]{2,1,0:T(8,128)(2,1)}), bf16[256,64,128]{2,1,0:T(8,128)(2,1)}) %all-gather.9.cloned.1.call-update) | async-done | bytes 4194320 | tf_op jit(solution)/shard_map/all_gather | solution.py:15
  192.4 34.2 %while.40 = (s32[]{:T(128)}, f32[8,64,128]{2,1,0:T(8,128)S(1)}, s32[]{:T(128)}, bf16[32,8]{1,0:T(8,128)(2,1)S(1)}, bf16[32,8,64,128]{3,2,1,0:T(8,128)(2,1)}, /*index=5*/s32[]{:T(128)}, s32[]{:T(128)}, s32[]{:T(128)}, s32[]{:T(128)}) while((s32[]{:T(128)}, f32[8,64,128]{2,1,0:T(8,128)S(1)}, s32[]{:T(128)}, ...), condition=%wide.region_1.2_spmd.clone, body=%wide.region_0.1_spmd.clone.sunk | while | flops 327696 | bytes 655607 | solution.py:33
  193.4 1.0 fusion.66
  194.5 1.0 fusion.66
  195.6 1.0 fusion.66
  196.7 1.0 fusion.66
  197.7 1.0 fusion.66
  207.4 1.0 fusion.66
  208.4 1.0 fusion.66
  217.0 1.0 fusion.66
  222.4 1.0 fusion.66
  227.0 1.6 fusion.15
  228.7 1.0 convolution_bitcast_fusion.2
  231.3 43.3 %all-gather.11.cloned.1.call-done = bf16[256,64,128]{2,1,0:T(8,128)(2,1)} async-done(((bf16[8,64,128]{2,1,0:T(8,128)(2,1)}), bf16[256,64,128]{2,1,0:T(8,128)(2,1)}) %all-gather.11.cloned.1.call-update) | async-done | bytes 4194320 | tf_op jit(solution)/shard_map/all_gather | solution.py:15
  274.7 33.7 %while.41 = (s32[]{:T(128)}, f32[8,64,128]{2,1,0:T(8,128)S(1)}, s32[]{:T(128)}, bf16[32,8]{1,0:T(8,128)(2,1)S(1)}, bf16[32,8,64,128]{3,2,1,0:T(8,128)(2,1)}, /*index=5*/s32[]{:T(128)}, s32[]{:T(128)}) while((s32[]{:T(128)}, f32[8,64,128]{2,1,0:T(8,128)S(1)}, s32[]{:T(128)}, bf16[32,8]{1,0:T(8,128)(2,1)S(1)}, ...), condition=%wide.region_7.8_spmd.clone, body=%wide.region_6.7_spmd.clone.sunk | while | flops 327692 | bytes 655545 | solution.py:33
  308.3 1.0 convolution_bitcast_fusion.1
  309.4 1.0 fusion.21
  310.5 7.8 %fusion.2 = bf16[8192,512]{0,1:T(8,128)(2,1)} fusion(bf16[256,512]{0,1:T(8,128)(2,1)S(1)} %bitcast.107, bf16[256,8192]{1,0:T(8,128)(2,1)} %param.10), kind=kOutput, calls=%fused_computation.7 | convolution fusion | flops 2151677952 | bytes 12845056 | tf_op jit(solution)/shard_map/dot_general | solution.py:108
  318.5 7.8 %convolution_convert_fusion.1 = bf16[256,8192]{1,0:T(8,128)(2,1)} fusion(bf16[256,512]{0,1:T(8,128)(2,1)S(1)} %bitcast.108, bf16[8192,512]{1,0:T(8,128)(2,1)} %all-gather.7.cloned.1.call-done), kind=kOutput, calls=%fused_computation.8 | convolution fusion | flops 2149580800 | bytes 12845056 | tf_op jit(solution)/shard_map/dot_general | solution.py:101
  326.3 46.5 %all-reduce.3.cloned.1.call-done = (bf16[256,128]{1,0:T(8,128)(2,1)}, bf16[256,128]{1,0:T(8,128)(2,1)}) async-done(((bf16[256,128]{1,0:T(8,128)(2,1)}, bf16[256,128]{1,0:T(8,128)(2,1)}), (bf16[256,128]{1,0:T(8,128)(2,1)}, bf16[256,128]{1,0:T(8,128)(2,1)})) %all-reduce.3.cloned.1.call-update) | async-done | bytes 131088 | tf_op jit(solution)/shard_map/psum | solution.py:98
  372.8 1.5 convert_element_type.131
  374.3 1.5 convert_element_type.135
  375.8 228.6 %reduce-scatter.5.cloned.1.call-done = bf16[256,512]{0,1:T(8,128)(2,1)} async-done(((bf16[8192,512]{0,1:T(8,128)(2,1)}), bf16[256,512]{0,1:T(8,128)(2,1)}) %reduce-scatter.5.cloned.1.call-update) | async-done | bytes 262160 | tf_op jit(solution)/shard_map/reduce_scatter | solution.py:107
  604.4 1.9 copy.31
  606.3 41.0 %reduce-scatter.3.cloned.1.call-done = bf16[256,1024]{1,0:T(8,128)(2,1)} async-done(((bf16[256,8192]{1,0:T(8,128)(2,1)}), bf16[256,1024]{1,0:T(8,128)(2,1)}) %reduce-scatter.3.cloned.1.call-update) | async-done | bytes 524304 | tf_op jit(solution)/shard_map/reduce_scatter | solution.py:104
  (149 shorter events, 61.2 us)
Async XLA Ops:
  7.2 42.2 %copy-start = (bf16[256,128]{1,0:T(8,128)(2,1)S(1)}, bf16[256,128]{1,0:T(8,128)(2,1)}, u32[]{:S(2)}) copy-start(bf16[256,128]{1,0:T(8,128)(2,1)} %param.13) | copy-start | bytes 196612
  7.2 105.4 %all-gather.7.cloned.1.call-start = ((), (), s32[]{:S(2)}) async-start(), calls=%async_computation.2 | async-start | bytes 8650752 | tf_op jit(solution)/shard_map/all_gather | solution.py:52
  7.9 184.5 %all-gather.9.cloned.1.call-start = ((), (), s32[]{:S(2)}) async-start(), calls=%async_computation.5 | async-start | bytes 4325376 | tf_op jit(solution)/shard_map/all_gather | solution.py:15
  12.2 262.5 %all-gather.11.cloned.1.call-start = ((), (), s32[]{:S(2)}) async-start(), calls=%async_computation.6 | async-start | bytes 4325376 | tf_op jit(solution)/shard_map/all_gather | solution.py:15
  120.8 252.0 %all-reduce.3.cloned.1.call-start = ((), (), s32[]{:S(2)}) async-start(), calls=%async_computation.7 | async-start | bytes 262144 | tf_op jit(solution)/shard_map/psum | solution.py:98
  226.6 3.8 copy-start.1
  310.4 294.0 %reduce-scatter.5.cloned.1.call-start = ((), (), s32[]{:S(2)}) async-start(), calls=%async_computation.4 | async-start | bytes 8650752 | tf_op jit(solution)/shard_map/reduce_scatter | solution.py:107
  318.3 329.0 %reduce-scatter.3.cloned.1.call-start = ((), (), s32[]{:S(2)}) async-start(), calls=%async_computation.3 | async-start | bytes 4718592 | tf_op jit(solution)/shard_map/reduce_scatter | solution.py:104
Sparse Core Ops, SparseCore 0:
  10.6 101.8 all-gather.6
  115.7 76.6 all-gather.8
  195.5 79.0 all-gather.10
  310.5 62.1 all-reduce.2
  377.2 227.1 reduce-scatter.4
  607.4 39.8 reduce-scatter.2

commit v2 on v0

v2 whole, which is shorter than its diff:
```python
import jax
import jax.numpy as jnp
from jax import lax
from jax.experimental import pallas as pl
from jax.experimental.pallas import tpu as pltpu
from jax.sharding import Mesh
from jax.sharding import PartitionSpec as P

NY, NZ, NX, NC = 4, 8, 4, 2
RUN = 256
HALF = RUN // 2
COLS = 512
HEADS = 8
DEPTH = 64
STATES = 128
QUARTER = 2048
SLICE = 1024
PACK = DEPTH + 32
F32, BF16 = jnp.float32, jnp.bfloat16
HIGH = lax.Precision.HIGHEST

M_W = 0
M_WS = M_W + 16
M_X = M_WS + 1
M_XS = M_X + 3
M_BACK = M_XS + 3
M_FORE = M_BACK + 17
M_G = M_FORE + 17
M_GS = M_G + 3
M_V = M_GS + 4
M_GW = M_V + 6
M_GI = M_GW + 16
M_T = M_GI + 6
M_S = M_T + 2
MESSAGES = M_S + 5


def dot(a, b, dims=((1,), (0,)), precision=None):
    return lax.dot_general(a, b, (dims, ((), ())), preferred_element_type=F32, precision=precision)


def kernel(
    x_hbm, w_ref, log_ref, b_ref, c_ref, dy_ref,
    gi_ref, gw_ref, gb_ref, gc_ref,
    wq, ws, xq, gq, gs, dec, gvi, grow_x, shrink_x, dg, xs, vals, gin, hin,
    b1, r1, b2, r2, b3, r3, f1, p1, f2, p2, f3, p3,
    acc, vs, vr, gws, gwr, gis, gir, gi_sum, gi_fin,
    sib_send, sib_recv, red, tot_send, tot_recv,
    send_sem, recv_sem, local_sem,
):
    y, z = lax.axis_index("y"), lax.axis_index("z")
    x, core = lax.axis_index("x"), lax.axis_index("core")
    other = 1 - core
    pending = []

    def message(src, dst, index, **to):
        return pltpu.make_async_remote_copy(
            src_ref=src, dst_ref=dst, send_sem=send_sem.at[index], recv_sem=recv_sem.at[index],
            device_id=to, device_id_type=pl.DeviceIdType.MESH,
        )

    def send(src, dst, index, **to):
        copy = message(src, dst, index, **to)
        copy.start()
        pending.append(copy)

    def arrived(dst, index, **to):
        message(dst, dst, index, **to).wait_recv()

    def rows(ref, start, size):
        return ref.at[pl.ds(pl.multiple_of(start, size), size), :]

    barrier = pltpu.get_barrier_semaphore()
    for d in range(1, NZ):
        pl.semaphore_signal(barrier, inc=1, device_id={"z": lax.rem(z + d, NZ)}, device_id_type=pl.DeviceIdType.MESH)
    for d in range(1, NY):
        pl.semaphore_signal(barrier, inc=1, device_id={"y": lax.rem(y + d, NY)}, device_id_type=pl.DeviceIdType.MESH)
    for d in range(1, NX):
        pl.semaphore_signal(barrier, inc=1, device_id={"x": lax.rem(x + d, NX)}, device_id_type=pl.DeviceIdType.MESH)
    pl.semaphore_signal(barrier, inc=1, device_id={"core": other}, device_id_type=pl.DeviceIdType.MESH)

    @pl.when(x != y)
    def _():
        pl.semaphore_signal(barrier, inc=1, device_id={"x": y, "y": x}, device_id_type=pl.DeviceIdType.MESH)

    own_x = pltpu.make_async_copy(
        x_hbm.at[:, pl.ds(pl.multiple_of(y * QUARTER, QUARTER), QUARTER)], rows(xq, y * RUN, RUN), local_sem
    )
    own_x.start()
    wq[pl.ds(pl.multiple_of(z * RUN, RUN), RUN), :] = w_ref[...]

    @pl.when(x == y)
    def _():
        pl.semaphore_wait(barrier, NZ + NY + NX - 2)

    @pl.when(x != y)
    def _():
        pl.semaphore_wait(barrier, NZ + NY + NX - 1)

    ring_z = (lax.rem(z + 1, NZ), lax.rem(z + NZ - 1, NZ))

    def w_part(shard, half):
        return rows(wq, shard * RUN + half * HALF, HALF)

    def w_send(way, hop, half):
        shard = lax.rem(z + NZ - (hop - 1), NZ) if way == 0 else lax.rem(z + (hop - 1), NZ)
        send(w_part(shard, half), w_part(shard, half), M_W + way * 8 + (hop - 1) * 2 + half, z=ring_z[way])

    def w_step(hop):
        for half in (0, 1):
            for way in (0, 1):
                if hop == NZ // 2 and half != way:
                    continue
                shard = lax.rem(z + NZ - hop, NZ) if way == 0 else lax.rem(z + hop, NZ)
                arrived(w_part(shard, half), M_W + way * 8 + (hop - 1) * 2 + half, z=ring_z[way])
                if hop < NZ // 2 - 1 or (hop == NZ // 2 - 1 and half == way):
                    w_send(way, hop + 1, half)

    for half in (0, 1):
        for way in (0, 1):
            w_send(way, 1, half)

    def x_part(row, col):
        return xq.at[
            pl.ds(pl.multiple_of(row * RUN, RUN), RUN), pl.ds(pl.multiple_of(col * SLICE, SLICE), SLICE)
        ]

    for d in (2, 1, 3):
        to = lax.rem(y + d, NY)
        send(
            x_hbm.at[:, pl.ds(pl.multiple_of(to * QUARTER + core * SLICE, SLICE), SLICE)],
            x_part(y, core), M_X + d - 1, y=to,
        )

    one = lax.broadcasted_iota(jnp.int32, (RUN, RUN), 0)
    two = lax.broadcasted_iota(jnp.int32, (RUN, RUN), 1)
    logs = log_ref[...]
    cum = dot((one >= two).astype(F32), logs, precision=HIGH)
    cum_t = dot(logs, (one <= two).astype(F32), ((0,), (0,)), HIGH)
    head_of = lax.broadcasted_iota(jnp.int32, (HEADS, COLS), 1) // DEPTH
    spread = (lax.broadcasted_iota(jnp.int32, (HEADS, COLS), 0) == head_of).astype(F32)
    cum_x = dot(cum, spread, precision=HIGH)
    grow_x[...] = jnp.exp(cum_x)
    shrink_x[...] = jnp.exp(cum_x[RUN - 1 :, :] - cum_x)
    dg[...] = (dy_ref[...].astype(F32) * grow_x[...]).astype(BF16)

    def scan_out(states, sent, got, base):
        for k in range(HEADS):
            sent[k, :DEPTH, :] = states[k * DEPTH : (k + 1) * DEPTH].astype(BF16)
            decay = jnp.exp(jnp.broadcast_to(cum[RUN - 1 :, k : k + 1], (16, STATES)))
            high = decay.astype(BF16)
            sent[k, DEPTH : DEPTH + 16, :] = high
            sent[k, DEPTH + 16 :, :] = (decay - high.astype(F32)).astype(BF16)
        for d in range(1, NZ):
            to = lax.rem(z + d, NZ)
            send(sent.at[to], got.at[z], base + d - 1, z=to)
        got[pl.ds(z, 1)] = sent[pl.ds(z, 1)]

    def unpack(ref, k):
        decay = ref[k, DEPTH : DEPTH + 16, :].astype(F32) + ref[k, DEPTH + 16 :, :].astype(F32)
        return ref[k, :DEPTH, :].astype(F32), decay[:1, :]

    def scan_rows(got, sent, got_y, base, order):
        for d in range(1, NZ):
            arrived(got.at[lax.rem(z + NZ - d, NZ)], base + d - 1, z=ring_z[0])
        carried, decays = jnp.zeros((DEPTH, STATES), F32), jnp.ones((1, STATES), F32)
        for k in order:
            state, decay = unpack(got, k)
            carried = decay * carried + state
            decays = decays * decay
        decays = jnp.broadcast_to(decays, (16, STATES))
        high = decays.astype(BF16)
        sent[:DEPTH, :] = carried.astype(BF16)
        sent[DEPTH : DEPTH + 16, :] = high
        sent[DEPTH + 16 :, :] = (decays - high.astype(F32)).astype(BF16)
        for d in range(1, NY):
            to = lax.rem(y + d, NY)
            send(sent, got_y.at[y], base + 7 + d - 1, y=to)
        got_y[pl.ds(y, 1)] = sent[...][None]

    def scan_back(got, got_y, sent, got_z, base, order, reverse):
        for d in range(1, NY):
            arrived(got_y.at[lax.rem(y + NY - d, NY)], base + 7 + d - 1, y=lax.rem(y + 1, NY))
        carried = jnp.zeros((DEPTH, STATES), F32)
        for k in reversed(range(NY)) if reverse else range(NY):
            state, decay = unpack(got_y, k)
            reached = (y < k) if reverse else (y > k)
            carried = jnp.where(reached, decay * carried + state, carried)
        for k in order:
            sent[k] = carried.astype(BF16)
            state, decay = unpack(got, k)
            carried = decay * carried + state
        for d in range(1, NZ):
            to = lax.rem(z + d, NZ)
            send(sent.at[to], got_z.at[z], base + 10 + d - 1, z=to)
        got_z[pl.ds(z, 1)] = sent[pl.ds(z, 1)]

    def scan_in(got_z, base, into):
        for d in range(1, NZ):
            arrived(got_z.at[lax.rem(z + NZ - d, NZ)], base + 10 + d - 1, z=ring_z[0])
        for k in range(HEADS):
            into[k * DEPTH : (k + 1) * DEPTH, :] = got_z[k]

    scan_out(dot(dg[...], c_ref[...], ((0,), (0,))), b1, r1, M_BACK)
    down, up = tuple(reversed(range(NZ))), tuple(range(NZ))

    scores = dot(b_ref[...], c_ref[...], ((1,), (1,)))
    low = lax.broadcasted_iota(jnp.int32, (RUN, 2 * DEPTH), 1) < DEPTH

    def within(pair):
        columns = slice(pair * 2 * DEPTH, (pair + 1) * 2 * DEPTH)
        part = dy_ref[:, columns]
        total = jnp.zeros((RUN, 2 * DEPTH), F32)
        for side in (0, 1):
            h = 2 * pair + side
            between = cum_t[h : h + 1, :] - cum[:, h : h + 1]
            decay = jnp.exp(jnp.where(two >= one, between, -1e30))
            dec[h] = decay
            kept = jnp.where(low if side == 0 else ~low, part, jnp.zeros_like(part))
            total = total + dot((decay * scores).astype(BF16), kept)
        gvi[:, columns] = total

    within(0)
    within(1)
    w_step(1)
    scan_rows(r1, b2, r2, M_BACK, down)
    within(2)
    within(3)
    w_step(2)
    scan_back(r1, r2, b3, r3, M_BACK, down, True)
    w_step(3)
    scan_in(r3, M_BACK, gin)

    def g_part(ref, row):
        return rows(ref, row * RUN, RUN)

    grad_values = gvi[...] + dot(b_ref[...], gin[...], ((1,), (1,))) * shrink_x[...]
    gq[pl.ds(pl.multiple_of(y * RUN, RUN), RUN), :] = grad_values.astype(BF16)
    for d in (2, 1, 3):
        send(g_part(gq, y), g_part(gq, y), M_G + d - 1, y=lax.rem(y + d, NY))
    send(g_part(gq, y), g_part(gs, y), M_GS, core=other)

    w_step(4)
    theirs = pl.multiple_of(other * SLICE, SLICE)
    mine = pl.multiple_of(core * SLICE, SLICE)
    send(wq.at[pl.ds(theirs, SLICE), :], ws, M_WS, core=other)
    for d in (1, 3, 2):
        part = x_part(lax.rem(y + NY - d, NY), core)
        arrived(part, M_X + d - 1, y=lax.rem(y + 1, NY))
        send(part, part, M_XS + d - 1, core=other)
    own_x.wait()
    for d in (1, 3, 2):
        source = lax.rem(y + NY - d, NY)
        arrived(g_part(gq, source), M_G + d - 1, y=lax.rem(y + 1, NY))
        send(g_part(gq, source), g_part(gs, source), M_GS + d, core=other)

    for d in range(1, NY):
        arrived(x_part(lax.rem(y + NY - d, NY), other), M_XS + d - 1, core=other)

    def gw_own(dest):
        columns = pl.ds(pl.multiple_of(dest * RUN, RUN), RUN)
        return dot(xq[:, columns], gq[...], ((0,), (0,)))

    def gw_step(t):
        for way in (0, 1):
            dest = lax.rem(z + 4 - t, NZ) if way == 0 else lax.rem(z + 4 + t, NZ)
            own = gw_own(dest)
            for half in (way, 1 - way):
                if t == 0 and half != way:
                    continue
                part = own[half * HALF : (half + 1) * HALF]
                index = way * 8 + t * 2 + half
                if t > 1 or (t == 1 and half == way):
                    arrived(gwr.at[way, t - 1, half], M_GW + index - 2, z=ring_z[way])
                    part = part + gwr[way, t - 1, half].astype(F32)
                gws[way, t, half] = part.astype(BF16)
                send(gws.at[way, t, half], gwr.at[way, t, half], M_GW + index, z=ring_z[way])

    def gw_end():
        own = gw_own(z)
        for half in (0, 1):
            part = own[half * HALF : (half + 1) * HALF]
            for way in (0, 1):
                arrived(gwr.at[way, 3, half], M_GW + way * 8 + 6 + half, z=ring_z[way])
                part = part + gwr[way, 3, half].astype(F32)
            gw_ref[half * HALF : (half + 1) * HALF, :] = part

    def four_step(t, axis, me, own, sent, got, base):
        ends = []
        for way in (0, 1):
            dest = lax.rem(me + 3 - t, 4) if way == 0 else lax.rem(me + 1 + t, 4)
            to = lax.rem(me + 1, 4) if way == 0 else lax.rem(me + 3, 4)
            part = own(dest, way)
            if t > 0:
                arrived(got.at[way, t - 1], base + way * 3 + t - 1, **{axis: to})
                part = part + got[way, t - 1].astype(F32)
            if t < 3:
                sent[way, t] = part.astype(BF16)
                send(sent.at[way, t], got.at[way, t], base + way * 3 + t, **{axis: to})
            ends.append(part)
        return ends

    def gi_own(dest, half):
        block = pl.ds(pl.multiple_of(dest * RUN + half * HALF, HALF), HALF)
        return dot(gq[block, :], wq[pl.ds(mine, SLICE), :], ((1,), (1,))) + dot(gs[block, :], ws[...], ((1,), (1,)))

    def gi_step(t):
        return four_step(t, "x", x, gi_own, gis, gir, M_GI)

    gw_step(0)
    arrived(ws, M_WS, core=other)
    for d in range(NY):
        arrived(g_part(gs, lax.rem(y + NY - d, NY)), M_GS + d, core=other)
    gi_step(0)

    def product(k, _):
        block = pl.ds(pl.multiple_of(k * RUN, RUN), RUN)
        acc[block, :] = dot(xq[block, :], wq[...])
        return 0

    lax.fori_loop(0, NY, product, 0)

    def v_own(dest, half):
        return acc[pl.ds(pl.multiple_of(dest * RUN + half * HALF, HALF), HALF), :]

    def v_step(t):
        return four_step(t, "y", y, v_own, vs, vr, M_V)

    v_step(0)
    gw_step(1)
    v_step(1)
    gi_step(1)
    v_step(2)
    gw_step(2)
    for half, part in enumerate(v_step(3)):
        vals[half * HALF : (half + 1) * HALF, :] = part.astype(BF16)
    xs[...] = (vals[...].astype(F32) * shrink_x[...]).astype(BF16)
    scan_out(dot(xs[...], b_ref[...], ((0,), (0,))), f1, p1, M_FORE)
    gi_step(2)
    gw_step(3)
    scan_rows(p1, f2, p2, M_FORE, up)

    mixed = jnp.zeros((RUN, RUN), F32)
    for pair in range(HEADS // 2):
        columns = slice(pair * 2 * DEPTH, (pair + 1) * 2 * DEPTH)
        part = vals[:, columns]
        for side in (0, 1):
            kept = jnp.where(low if side == 0 else ~low, part, jnp.zeros_like(part))
            mixed = mixed + dec[2 * pair + side] * dot(kept, dy_ref[:, columns], ((1,), (1,)))
    mixed = mixed.astype(BF16)
    grad_b = dot(mixed, c_ref[...]) + dot(xs[...], gin[...])
    grad_c = dot(mixed, b_ref[...], ((0,), (0,)))
    scan_back(p1, p2, f3, p3, M_FORE, up, False)

    for half, part in enumerate(gi_step(3)):
        gi_sum[half * HALF : (half + 1) * HALF, :] = part.astype(BF16)

        @pl.when(x != y)
        def _(half=half):
            block = pl.ds(half * HALF, HALF)
            message(gi_sum.at[block, :], gi_fin.at[block, :], M_T + half, x=y, y=x).start()

    scan_in(p3, M_FORE, hin)
    grad_c = grad_c + dot(dg[...], hin[...])

    sib_send[...] = jnp.where(core == 0, grad_c, grad_b)
    send(sib_send, sib_recv, M_S, core=other)
    arrived(sib_recv, M_S, core=other)
    red[pl.ds(x, 1)] = (jnp.where(core == 0, grad_b, grad_c) + sib_recv[...]).astype(BF16)[None]
    for d in range(1, NX):
        send(red.at[x], red.at[x], M_S + d, x=lax.rem(x + d, NX))
    gw_end()
    for d in range(1, NX):
        arrived(red.at[lax.rem(x + NX - d, NX)], M_S + d, x=lax.rem(x + 1, NX))
    total = red[0].astype(F32)
    for k in range(1, NX):
        total = total + red[k].astype(F32)
    tot_send[...] = total
    send(tot_send, tot_recv, M_S + 4, core=other)
    arrived(tot_recv, M_S + 4, core=other)
    gb_ref[...] = jnp.where(core == 0, tot_send[...], tot_recv[...])
    gc_ref[...] = jnp.where(core == 0, tot_recv[...], tot_send[...])

    @pl.when(x != y)
    def _():
        for half in (0, 1):
            block = pl.ds(half * HALF, HALF)
            copy = message(gi_sum.at[block, :], gi_fin.at[block, :], M_T + half, x=y, y=x)
            copy.wait_send()
            copy.wait_recv()
        gi_ref[...] = gi_fin[...]

    @pl.when(x == y)
    def _():
        gi_ref[...] = gi_sum[...]

    for copy in pending:
        copy.wait_send()


def per_device(inputs, w_value, log_decay, b_proj, c_proj, grad_out):
    vmem = pl.BlockSpec(memory_space=pltpu.VMEM)

    def pair(count, *rest):
        return [pltpu.VMEM((count, *rest), BF16)] * 2

    scan = [
        *pair(HEADS, PACK, STATES),
        pltpu.VMEM((PACK, STATES), BF16),
        pltpu.VMEM((NY, PACK, STATES), BF16),
        *pair(HEADS, DEPTH, STATES),
    ]
    return pl.pallas_call(
        kernel,
        out_shape=(
            jax.ShapeDtypeStruct((RUN, SLICE), BF16),
            jax.ShapeDtypeStruct((RUN, COLS), F32),
            jax.ShapeDtypeStruct((RUN, STATES), F32),
            jax.ShapeDtypeStruct((RUN, STATES), F32),
        ),
        in_specs=[pl.BlockSpec(memory_space=pl.ANY), vmem, vmem, vmem, vmem, vmem],
        out_specs=(vmem, vmem, vmem, vmem),
        scratch_shapes=[
            pltpu.VMEM((QUARTER, COLS), BF16),
            pltpu.VMEM((SLICE, COLS), BF16),
            pltpu.VMEM((NY * RUN, QUARTER), BF16),
            pltpu.VMEM((NY * RUN, COLS), BF16),
            pltpu.VMEM((NY * RUN, COLS), BF16),
            pltpu.VMEM((HEADS, RUN, RUN), F32),
            pltpu.VMEM((RUN, COLS), F32),
            pltpu.VMEM((RUN, COLS), F32),
            pltpu.VMEM((RUN, COLS), F32),
            pltpu.VMEM((RUN, COLS), BF16),
            pltpu.VMEM((RUN, COLS), BF16),
            pltpu.VMEM((RUN, COLS), BF16),
            pltpu.VMEM((HEADS * DEPTH, STATES), BF16),
            pltpu.VMEM((HEADS * DEPTH, STATES), BF16),
            *scan,
            *scan,
            pltpu.VMEM((NY * RUN, COLS), F32),
            *pair(2, 3, HALF, COLS),
            *pair(2, 4, 2, HALF, COLS),
            *pair(2, 3, HALF, SLICE),
            *pair(RUN, SLICE),
            pltpu.VMEM((RUN, STATES), F32),
            pltpu.VMEM((RUN, STATES), F32),
            pltpu.VMEM((NX, RUN, STATES), BF16),
            pltpu.VMEM((RUN, STATES), F32),
            pltpu.VMEM((RUN, STATES), F32),
            pltpu.SemaphoreType.DMA((MESSAGES,)),
            pltpu.SemaphoreType.DMA((MESSAGES,)),
            pltpu.SemaphoreType.DMA,
        ],
        compiler_params=pltpu.CompilerParams(
            collective_id=0, has_side_effects=True, vmem_limit_bytes=56 * 2**20
        ),
        name="ssd_backward",
    )(inputs, w_value, log_decay, b_proj, c_proj, grad_out)


def solution(mesh):
    grid = Mesh(mesh.devices.reshape(NY, NZ, NX, NC), ("y", "z", "x", "core"))
    seq, head = ("y", "z"), ("x", "core")
    placed = (P(seq, None), P(seq, head), P(seq, head), P(seq, None), P(seq, None), P(seq, head))
    return jax.shard_map(
        per_device,
        mesh=grid,
        in_specs=placed,
        out_specs=(P(seq, head), P(seq, head), P(seq, None), P(seq, None)),
        check_vma=False,
    )
```

time: 657 us -> 130 us (0.20)
  waiting for transfers between devices: 493 us -> 0 us
  Pallas kernels: 0 us -> 121 us
  other arithmetic: 70.2 us -> 0 us
  blocking collectives: 37.4 us -> 0 us
  matrix products: 33.2 us -> 0 us
  between operations: 14.2 us -> 0.64 us
    reduce_scatter x2 -> x0, waiting for transfers between devices: 270 us -> none  [the longest x1 229 us: per_device(): lax.psum_scatter(lax.dot_general(inputs, grad_values, (((0,), (0,)), ((),...]
    all_gather x3 -> x0, waiting for transfers between devices: 176 us -> none  [the longest x2 115 us: carried_in(): lax.all_gather(part.astype(kind), axis)]
    pallas_call x0 -> x1, Pallas kernels: none -> 121 us  [per_device(): pl.pallas_call(kernel, out_shape=(jax.ShapeDtypeStruct((RUN, SLICE), BF16...]
    select_n x64 -> x0, other arithmetic: 64.9 us -> none  [lap(): return jax.tree.map(lambda a, b: jnp.where(reached, a, b), new, before)]
    psum x1 -> x0, waiting for transfers between devices: 46.5 us -> none  [per_device(): lax.psum(grad_b.reshape(steps, states).astype(jnp.bfloat16), 'head')]
    all_gather x1 -> x0, blocking collectives: 37.4 us -> none  [carried_in(): lax.all_gather(part.astype(kind), axis)]
    dot_general x13 -> x0, matrix products: 33.2 us -> none  [the longest x1 7.77 us: per_device(): lax.dot_general(inputs, grad_values, (((0,), (0,)), ((), ())), preferred_...]
  transfers between devices with their start and end apart: 6 -> 0, of which waited for: 6 -> 0; matrix products, arithmetic and copies ran while one was open for 11% -> 0% of each run, Pallas kernels for 0% -> 0%
where the time goes in v2:
time: 130 us
  Pallas kernels  121 us (93%)
  local copies, waits for them, and re-layouts  8.36 us (6%)
    pallas_call x1, Pallas kernels, per_device(): pl.pallas_call(kernel, out_shape=(jax.ShapeDtypeStruct((RUN, SLICE), BF16...  121 us
    unnamed x5, local copies, waits for them, and re-layouts  8.36 us

profile of v2, /device:TPU:1, one launch (start us, length us, event | category | flops | bytes accessed | tf_op | source)
XLA Modules:
  0.0 130.0 jit_solution(4411925029417562917)
XLA Ops:
  0.6 1.5 %copy.10.log_ref = f32[256,8]{1,0:T(8,128)} copy(f32[256,8]{0,1:T(8,128)} %param.8) | data formatting | bytes 16384 | tf_op args[2]
  2.1 121.0 %ssd_backward.1 = (bf16[256,1024]{1,0:T(8,128)(2,1)}, f32[256,512]{1,0:T(8,128)}, f32[256,128]{1,0:T(8,128)}, f32[256,128]{1,0:T(8,128)}) custom-call(bf16[256,8192]{1,0:T(8,128)(2,1)} %x_hbm.1, bf16[256,512]{1,0:T(8,128)(2,1)} %w_ref.1, f32[256,8]{1,0:T(8,128)} %copy.10.log_ref, bf16[256,128]{1,0:T(8,128)(2,1)} %b_ref.1, bf16[256,128]{1,0:T(8,128)(2,1)} %c_ref.1, ...), custom_call_target="tpu_custom_call" | custom-call | tf_op jit(solution)/shard_map/ssd_backward/pallas_call | solution.py:413
  123.1 1.9 %copy.15 = bf16[256,1024]{1,0:T(8,128)(2,1)} copy(bf16[256,1024]{1,0:T(8,128)(2,1)} %get-tuple-element.8) | data formatting | bytes 1048576
  125.0 1.9 %copy.16 = f32[256,512]{1,0:T(8,128)} copy(f32[256,512]{1,0:T(8,128)} %get-tuple-element.9) | data formatting | bytes 1048576
  126.8 1.6 %copy.17 = f32[256,128]{1,0:T(8,128)} copy(f32[256,128]{1,0:T(8,128)} %get-tuple-element.10) | data formatting | bytes 262144
  128.4 1.6 %copy.18 = f32[256,128]{1,0:T(8,128)} copy(f32[256,128]{1,0:T(8,128)} %get-tuple-element.11) | data formatting | bytes 262144

commit v3 on v2

--- a/solution.py
+++ b/solution.py
@@ -15,6 +15,8 @@
 STATES = 128
 QUARTER = 2048
 SLICE = 1024
+SUB = 256
+PIECE = 64
 PACK = DEPTH + 32
 F32, BF16 = jnp.float32, jnp.bfloat16
 HIGH = lax.Precision.HIGHEST
@@ -22,16 +24,17 @@
 M_W = 0
 M_WS = M_W + 16
 M_X = M_WS + 1
-M_XS = M_X + 3
+M_XX = M_X + 3
+M_XS = M_XX + 9
 M_BACK = M_XS + 3
 M_FORE = M_BACK + 17
 M_G = M_FORE + 17
 M_GS = M_G + 3
 M_V = M_GS + 4
 M_GW = M_V + 6
-M_GI = M_GW + 16
-M_T = M_GI + 6
-M_S = M_T + 2
+M_C = M_GW + 16
+M_D = M_C + 16
+M_S = M_D + 4
 MESSAGES = M_S + 5
 
 
@@ -40,11 +43,11 @@
 
 
 def kernel(
-    x_hbm, w_ref, log_ref, b_ref, c_ref, dy_ref,
+    x_hbm, w_ref, log_t_ref, b_ref, c_ref, dy_ref,
     gi_ref, gw_ref, gb_ref, gc_ref,
     wq, ws, xq, gq, gs, dec, gvi, grow_x, shrink_x, dg, xs, vals, gin, hin,
     b1, r1, b2, r2, b3, r3, f1, p1, f2, p2, f3, p3,
-    acc, vs, vr, gws, gwr, gis, gir, gi_sum, gi_fin,
+    acc, gia, vs, vr, gws, gwr, gis, gir, gi_fin,
     sib_send, sib_recv, red, tot_send, tot_recv,
     send_sem, recv_sem, local_sem,
 ):
@@ -53,9 +56,9 @@
     other = 1 - core
     pending = []
 
-    def message(src, dst, index, **to):
+    def message(src, dst, index, at=None, **to):
         return pltpu.make_async_remote_copy(
-            src_ref=src, dst_ref=dst, send_sem=send_sem.at[index], recv_sem=recv_sem.at[index],
+            src_ref=src, dst_ref=dst, send_sem=send_sem.at[index], recv_sem=recv_sem.at[index if at is None else at],
             device_id=to, device_id_type=pl.DeviceIdType.MESH,
         )
 
@@ -79,23 +82,41 @@
         pl.semaphore_signal(barrier, inc=1, device_id={"x": lax.rem(x + d, NX)}, device_id_type=pl.DeviceIdType.MESH)
     pl.semaphore_signal(barrier, inc=1, device_id={"core": other}, device_id_type=pl.DeviceIdType.MESH)
 
-    @pl.when(x != y)
-    def _():
-        pl.semaphore_signal(barrier, inc=1, device_id={"x": y, "y": x}, device_id_type=pl.DeviceIdType.MESH)
-
     own_x = pltpu.make_async_copy(
         x_hbm.at[:, pl.ds(pl.multiple_of(y * QUARTER, QUARTER), QUARTER)], rows(xq, y * RUN, RUN), local_sem
     )
     own_x.start()
     wq[pl.ds(pl.multiple_of(z * RUN, RUN), RUN), :] = w_ref[...]
 
-    @pl.when(x == y)
-    def _():
-        pl.semaphore_wait(barrier, NZ + NY + NX - 2)
-
-    @pl.when(x != y)
-    def _():
-        pl.semaphore_wait(barrier, NZ + NY + NX - 1)
+    one = lax.broadcasted_iota(jnp.int32, (RUN, RUN), 0)
+    two = lax.broadcasted_iota(jnp.int32, (RUN, RUN), 1)
+    logs = log_t_ref[...]
+    cum = dot((one >= two).astype(F32), logs, ((1,), (1,)), HIGH)
+    cum_t = dot(logs, (one <= two).astype(F32), precision=HIGH)
+    head_of = lax.broadcasted_iota(jnp.int32, (HEADS, COLS), 1) // DEPTH
+    spread = (lax.broadcasted_iota(jnp.int32, (HEADS, COLS), 0) == head_of).astype(F32)
+    cum_x = dot(cum, spread, precision=HIGH)
+    grow_x[...] = jnp.exp(cum_x)
+    shrink_x[...] = jnp.exp(cum_x[RUN - 1 :, :] - cum_x)
+    dg[...] = (dy_ref[...].astype(F32) * grow_x[...]).astype(BF16)
+
+    def scan_pack(states, sent):
+        for k in range(HEADS):
+            sent[k, :DEPTH, :] = states[k * DEPTH : (k + 1) * DEPTH].astype(BF16)
+            decay = jnp.exp(jnp.broadcast_to(cum[RUN - 1 :, k : k + 1], (16, STATES)))
+            high = decay.astype(BF16)
+            sent[k, DEPTH : DEPTH + 16, :] = high
+            sent[k, DEPTH + 16 :, :] = (decay - high.astype(F32)).astype(BF16)
+
+    def scan_out(sent, got, base):
+        for d in (4, 3, 5, 2, 6, 1, 7):
+            to = lax.rem(z + d, NZ)
+            send(sent.at[to], got.at[z], base + d - 1, z=to)
+        got[pl.ds(z, 1)] = sent[pl.ds(z, 1)]
+
+    scan_pack(dot(dg[...], c_ref[...], ((0,), (0,))), b1)
+    pl.semaphore_wait(barrier, NZ + NY + NX - 2)
+    scan_out(b1, r1, M_BACK)
 
     ring_z = (lax.rem(z + 1, NZ), lax.rem(z + NZ - 1, NZ))
 
@@ -125,36 +146,29 @@
             pl.ds(pl.multiple_of(row * RUN, RUN), RUN), pl.ds(pl.multiple_of(col * SLICE, SLICE), SLICE)
         ]
 
+    def x_piece(row, sub):
+        return xq.at[
+            pl.ds(pl.multiple_of(row * RUN, RUN), RUN), pl.ds(pl.multiple_of(core * SLICE + sub * SUB, SUB), SUB)
+        ]
+
     for d in (2, 1, 3):
         to = lax.rem(y + d, NY)
-        send(
-            x_hbm.at[:, pl.ds(pl.multiple_of(to * QUARTER + core * SLICE, SLICE), SLICE)],
-            x_part(y, core), M_X + d - 1, y=to,
-        )
-
-    one = lax.broadcasted_iota(jnp.int32, (RUN, RUN), 0)
-    two = lax.broadcasted_iota(jnp.int32, (RUN, RUN), 1)
-    logs = log_ref[...]
-    cum = dot((one >= two).astype(F32), logs, precision=HIGH)
-    cum_t = dot(logs, (one <= two).astype(F32), ((0,), (0,)), HIGH)
-    head_of = lax.broadcasted_iota(jnp.int32, (HEADS, COLS), 1) // DEPTH
-    spread = (lax.broadcasted_iota(jnp.int32, (HEADS, COLS), 0) == head_of).astype(F32)
-    cum_x = dot(cum, spread, precision=HIGH)
-    grow_x[...] = jnp.exp(cum_x)
-    shrink_x[...] = jnp.exp(cum_x[RUN - 1 :, :] - cum_x)
-    dg[...] = (dy_ref[...].astype(F32) * grow_x[...]).astype(BF16)
-
-    def scan_out(states, sent, got, base):
-        for k in range(HEADS):
-            sent[k, :DEPTH, :] = states[k * DEPTH : (k + 1) * DEPTH].astype(BF16)
-            decay = jnp.exp(jnp.broadcast_to(cum[RUN - 1 :, k : k + 1], (16, STATES)))
-            high = decay.astype(BF16)
-            sent[k, DEPTH : DEPTH + 16, :] = high
-            sent[k, DEPTH + 16 :, :] = (decay - high.astype(F32)).astype(BF16)
-        for d in range(1, NZ):
-            to = lax.rem(z + d, NZ)
-            send(sent.at[to], got.at[z], base + d - 1, z=to)
-        got[pl.ds(z, 1)] = sent[pl.ds(z, 1)]
+        columns = pl.ds(pl.multiple_of(to * QUARTER + core * SLICE + x * SUB, SUB), SUB)
+        send(x_hbm.at[:, columns], x_piece(y, x), M_X + d - 1, y=to)
+
+    def x_relay():
+        for d in (1, 3, 2):
+            source = lax.rem(y + NY - d, NY)
+            arrived(x_piece(source, x), M_X + d - 1, y=lax.rem(y + 1, NY))
+            for e in (2, 1, 3):
+                send(x_piece(source, x), x_piece(source, x), M_XX + (d - 1) * 3 + e - 1, x=lax.rem(x + e, NX))
+
+    def x_collect():
+        for d in (1, 3, 2):
+            source = lax.rem(y + NY - d, NY)
+            for e in (1, 2, 3):
+                arrived(x_piece(source, lax.rem(x + NX - e, NX)), M_XX + (d - 1) * 3 + e - 1, x=lax.rem(x + 1, NX))
+            send(x_part(source, core), x_part(source, core), M_XS + d - 1, core=other)
 
     def unpack(ref, k):
         decay = ref[k, DEPTH : DEPTH + 16, :].astype(F32) + ref[k, DEPTH + 16 :, :].astype(F32)
@@ -201,7 +215,6 @@
         for k in range(HEADS):
             into[k * DEPTH : (k + 1) * DEPTH, :] = got_z[k]
 
-    scan_out(dot(dg[...], c_ref[...], ((0,), (0,))), b1, r1, M_BACK)
     down, up = tuple(reversed(range(NZ))), tuple(range(NZ))
 
     scores = dot(b_ref[...], c_ref[...], ((1,), (1,)))
@@ -224,6 +237,7 @@
     within(1)
     w_step(1)
     scan_rows(r1, b2, r2, M_BACK, down)
+    x_relay()
     within(2)
     within(3)
     w_step(2)
@@ -244,16 +258,12 @@
     theirs = pl.multiple_of(other * SLICE, SLICE)
     mine = pl.multiple_of(core * SLICE, SLICE)
     send(wq.at[pl.ds(theirs, SLICE), :], ws, M_WS, core=other)
-    for d in (1, 3, 2):
-        part = x_part(lax.rem(y + NY - d, NY), core)
-        arrived(part, M_X + d - 1, y=lax.rem(y + 1, NY))
-        send(part, part, M_XS + d - 1, core=other)
+    x_collect()
     own_x.wait()
     for d in (1, 3, 2):
         source = lax.rem(y + NY - d, NY)
         arrived(g_part(gq, source), M_G + d - 1, y=lax.rem(y + 1, NY))
         send(g_part(gq, source), g_part(gs, source), M_GS + d, core=other)
-
     for d in range(1, NY):
         arrived(x_part(lax.rem(y + NY - d, NY), other), M_XS + d - 1, core=other)
 
@@ -300,18 +310,61 @@
             ends.append(part)
         return ends
 
-    def gi_own(dest, half):
-        block = pl.ds(pl.multiple_of(dest * RUN + half * HALF, HALF), HALF)
-        return dot(gq[block, :], wq[pl.ds(mine, SLICE), :], ((1,), (1,))) + dot(gs[block, :], ws[...], ((1,), (1,)))
-
-    def gi_step(t):
-        return four_step(t, "x", x, gi_own, gis, gir, M_GI)
+    turn = lax.rem(x + NX - y, NX)
+
+    def gi_rows(block, way, sub):
+        return pl.ds(pl.multiple_of(block * RUN + way * HALF + sub * PIECE, PIECE), PIECE)
+
+    def gi_product(d):
+        block = pl.ds(pl.multiple_of(lax.rem(y + d, NY) * RUN, RUN), RUN)
+        gia[block, :] = dot(gq[block, :], wq[pl.ds(mine, SLICE), :], ((1,), (1,))) + dot(
+            gs[block, :], ws[...], ((1,), (1,))
+        )
+
+    def chain(slot):
+        for way in (0, 1):
+            place = lax.rem(turn + 3, NX) if way == 0 else lax.rem(7 - turn, NX)
+            to = lax.rem(x + 1, NX) if way == 0 else lax.rem(x + 3, NX)
+            i = slot - place
+
+            @pl.when((i >= 0) & (i < 8))
+            def _(way=way, place=place, to=to, i=i):
+                block, sub = lax.rem(y + lax.div(i, 2), NY), lax.rem(i, 2)
+                index = M_C + way * 8 + i
+                own = gia[gi_rows(block, way, sub), :]
+
+                @pl.when(place == 0)
+                def _():
+                    gis[way, pl.ds(i, 1)] = own.astype(BF16)[None]
+
+                @pl.when(place > 0)
+                def _():
+                    arrived(gir.at[way, i], index, x=to)
+                    gis[way, pl.ds(i, 1)] = (own[None] + gir[way, pl.ds(i, 1)].astype(F32)).astype(BF16)
+
+                @pl.when(place < 3)
+                def _():
+                    message(gis.at[way, i], gir.at[way, i], index, x=to).start()
+
+                @pl.when((place == 3) & (i < 2))
+                def _():
+                    gi_fin[gi_rows(0, way, sub), :] = gis[way, pl.ds(i, 1)][0]
+
+                @pl.when((place == 3) & (i >= 2))
+                def _():
+                    message(
+                        gis.at[way, i], gi_fin.at[gi_rows(0, way, sub), :], index, M_D + way * 2 + sub, y=block
+                    ).start()
 
     gw_step(0)
     arrived(ws, M_WS, core=other)
     for d in range(NY):
         arrived(g_part(gs, lax.rem(y + NY - d, NY)), M_GS + d, core=other)
-    gi_step(0)
+    gi_product(0)
+    chain(0)
+    gi_product(1)
+    gi_product(2)
+    gi_product(3)
 
     def product(k, _):
         block = pl.ds(pl.multiple_of(k * RUN, RUN), RUN)
@@ -327,17 +380,22 @@
         return four_step(t, "y", y, v_own, vs, vr, M_V)
 
     v_step(0)
+    chain(1)
     gw_step(1)
+    chain(2)
     v_step(1)
-    gi_step(1)
+    chain(3)
     v_step(2)
     gw_step(2)
+    chain(4)
     for half, part in enumerate(v_step(3)):
         vals[half * HALF : (half + 1) * HALF, :] = part.astype(BF16)
     xs[...] = (vals[...].astype(F32) * shrink_x[...]).astype(BF16)
-    scan_out(dot(xs[...], b_ref[...], ((0,), (0,))), f1, p1, M_FORE)
-    gi_step(2)
+    scan_pack(dot(xs[...], b_ref[...], ((0,), (0,))), f1)
+    scan_out(f1, p1, M_FORE)
+    chain(5)
     gw_step(3)
+    chain(6)
     scan_rows(p1, f2, p2, M_FORE, up)
 
     mixed = jnp.zeros((RUN, RUN), F32)
@@ -350,16 +408,11 @@
     mixed = mixed.astype(BF16)
     grad_b = dot(mixed, c_ref[...]) + dot(xs[...], gin[...])
     grad_c = dot(mixed, b_ref[...], ((0,), (0,)))
+    chain(7)
     scan_back(p1, p2, f3, p3, M_FORE, up, False)
-
-    for half, part in enumerate(gi_step(3)):
-        gi_sum[half * HALF : (half + 1) * HALF, :] = part.astype(BF16)
-
-        @pl.when(x != y)
-        def _(half=half):
-            block = pl.ds(half * HALF, HALF)
-            message(gi_sum.at[block, :], gi_fin.at[block, :], M_T + half, x=y, y=x).start()
-
+    chain(8)
+    gw_end()
+    chain(9)
     scan_in(p3, M_FORE, hin)
     grad_c = grad_c + dot(dg[...], hin[...])
 
@@ -369,7 +422,7 @@
     red[pl.ds(x, 1)] = (jnp.where(core == 0, grad_b, grad_c) + sib_recv[...]).astype(BF16)[None]
     for d in range(1, NX):
         send(red.at[x], red.at[x], M_S + d, x=lax.rem(x + d, NX))
-    gw_end()
+    chain(10)
     for d in range(1, NX):
         arrived(red.at[lax.rem(x + NX - d, NX)], M_S + d, x=lax.rem(x + 1, NX))
     total = red[0].astype(F32)
@@ -383,19 +436,26 @@
 
     @pl.when(x != y)
     def _():
-        for half in (0, 1):
-            block = pl.ds(half * HALF, HALF)
-            copy = message(gi_sum.at[block, :], gi_fin.at[block, :], M_T + half, x=y, y=x)
-            copy.wait_send()
-            copy.wait_recv()
-        gi_ref[...] = gi_fin[...]
-
-    @pl.when(x == y)
-    def _():
-        gi_ref[...] = gi_sum[...]
+        for way in (0, 1):
+            for sub in (0, 1):
+                arrived(gi_fin.at[gi_rows(0, way, sub), :], M_D + way * 2 + sub, y=x)
+
+    gi_ref[...] = gi_fin[...]
+    for way in (0, 1):
+        for i in range(8):
+            sent = message(gis.at[way, i], gir.at[way, i], M_C + way * 8 + i, x=lax.rem(x + 1, NX))
+            if i >= 2:
+                sent.wait_send()
+            else:
+                pl.when(x != y)(sent.wait_send)
 
     for copy in pending:
         copy.wait_send()
+
+
+def hand_over(*refs):
+    for source, result in zip(refs[:4], refs[4:], strict=True):
+        result[...] = source[...]
 
 
 def per_device(inputs, w_value, log_decay, b_proj, c_proj, grad_out):
@@ -410,7 +470,7 @@
         pltpu.VMEM((NY, PACK, STATES), BF16),
         *pair(HEADS, DEPTH, STATES),
     ]
-    return pl.pallas_call(
+    results = pl.pallas_call(
         kernel,
         out_shape=(
             jax.ShapeDtypeStruct((RUN, SLICE), BF16),
@@ -438,10 +498,11 @@
             *scan,
             *scan,
             pltpu.VMEM((NY * RUN, COLS), F32),
+            pltpu.VMEM((NY * RUN, SLICE), F32),
             *pair(2, 3, HALF, COLS),
             *pair(2, 4, 2, HALF, COLS),
-            *pair(2, 3, HALF, SLICE),
-            *pair(RUN, SLICE),
+            *pair(2, 8, PIECE, SLICE),
+            pltpu.VMEM((RUN, SLICE), BF16),
             pltpu.VMEM((RUN, STATES), F32),
             pltpu.VMEM((RUN, STATES), F32),
             pltpu.VMEM((NX, RUN, STATES), BF16),
@@ -455,7 +516,14 @@
             collective_id=0, has_side_effects=True, vmem_limit_bytes=56 * 2**20
         ),
         name="ssd_backward",
-    )(inputs, w_value, log_decay, b_proj, c_proj, grad_out)
+    )(inputs, w_value, log_decay.T, b_proj, c_proj, grad_out)
+    return pl.pallas_call(
+        hand_over,
+        out_shape=tuple(jax.ShapeDtypeStruct(r.shape, r.dtype) for r in results),
+        in_specs=[vmem] * 4,
+        out_specs=(vmem,) * 4,
+        name="hand_over",
+    )(*results)
 
 
 def solution(mesh):

time: 130 us -> 113 us (0.87)
  local copies, waits for them, and re-layouts: 8.36 us -> 0 us
  Pallas kernels: 121 us -> 113 us
    pallas_call x1, Pallas kernels: 121 us -> 110 us  [per_device(): pl.pallas_call(kernel, out_shape=(jax.ShapeDtypeStruct((RUN, SLICE), BF16...]
    unnamed x5 -> x0, local copies, waits for them, and re-layouts: 8.36 us -> none
    pallas_call x0 -> x1, Pallas kernels: none -> 2.34 us  [per_device(): pl.pallas_call(hand_over, out_shape=tuple((jax.ShapeDtypeStruct(r.shape,...]
where the time goes in v3:
time: 113 us
  Pallas kernels  113 us (100%)
    pallas_call x1, Pallas kernels, per_device(): pl.pallas_call(kernel, out_shape=(jax.ShapeDtypeStruct((RUN, SLICE), BF16...  110 us
    pallas_call x1, Pallas kernels, per_device(): pl.pallas_call(hand_over, out_shape=tuple((jax.ShapeDtypeStruct(r.shape,...  2.34 us

profile of v3, /device:TPU:1, one launch (start us, length us, event | category | flops | bytes accessed | tf_op | source)
XLA Modules:
  0.0 113.1 jit_solution(8419260867007057141)
XLA Ops:
  0.6 110.2 %ssd_backward.1 = (bf16[256,1024]{1,0:T(8,128)(2,1)}, f32[256,512]{1,0:T(8,128)}, f32[256,128]{1,0:T(8,128)}, f32[256,128]{1,0:T(8,128)}) custom-call(bf16[256,8192]{1,0:T(8,128)(2,1)} %x_hbm.1, bf16[256,512]{1,0:T(8,128)(2,1)} %w_ref.1, f32[8,256]{1,0:T(8,128)} %bitcast.1, bf16[256,128]{1,0:T(8,128)(2,1)} %b_ref.1, bf16[256,128]{1,0:T(8,128)(2,1)} %c_ref.1, ...), custom_call_target="tpu_custom_call" | custom-call | tf_op jit(solution)/shard_map/ssd_backward/pallas_call | solution.py:473
  110.8 2.3 %hand_over.1 = (bf16[256,1024]{1,0:T(8,128)(2,1)}, f32[256,512]{1,0:T(8,128)}, f32[256,128]{1,0:T(8,128)}, f32[256,128]{1,0:T(8,128)}) custom-call(bf16[256,1024]{1,0:T(8,128)(2,1)} %get-tuple-element.8.refs_0_, f32[256,512]{1,0:T(8,128)} %get-tuple-element.9.refs_1_, f32[256,128]{1,0:T(8,128)} %get-tuple-element.10.refs_2_, ...), custom_call_target="tpu_custom_call" | custom-call | tf_op jit(solution)/shard_map/hand_over/pallas_call | solution.py:520

commit v4 on v3

--- a/solution.py
+++ b/solution.py
@@ -16,8 +16,9 @@
 QUARTER = 2048
 SLICE = 1024
 SUB = 256
+EIGHTH = RUN // 8
 PIECE = 64
-PACK = DEPTH + 32
+PACK = DEPTH + 16
 F32, BF16 = jnp.float32, jnp.bfloat16
 HIGH = lax.Precision.HIGHEST
 
@@ -31,11 +32,11 @@
 M_G = M_FORE + 17
 M_GS = M_G + 3
 M_V = M_GS + 4
-M_GW = M_V + 6
+M_GW = M_V + 3
 M_C = M_GW + 16
 M_D = M_C + 16
 M_S = M_D + 4
-MESSAGES = M_S + 5
+MESSAGES = M_S + 14
 
 
 def dot(a, b, dims=((1,), (0,)), precision=None):
@@ -48,7 +49,7 @@
     wq, ws, xq, gq, gs, dec, gvi, grow_x, shrink_x, dg, xs, vals, gin, hin,
     b1, r1, b2, r2, b3, r3, f1, p1, f2, p2, f3, p3,
     acc, gia, vs, vr, gws, gwr, gis, gir, gi_fin,
-    sib_send, sib_recv, red, tot_send, tot_recv,
+    part_send, part_recv, sums,
     send_sem, recv_sem, local_sem,
 ):
     y, z = lax.axis_index("y"), lax.axis_index("z")
@@ -73,15 +74,19 @@
     def rows(ref, start, size):
         return ref.at[pl.ds(pl.multiple_of(start, size), size), :]
 
+    me = x * NC + core
+
+    def group_peer(e):
+        to = lax.rem(me + e, NX * NC)
+        return {"x": lax.div(to, NC), "core": lax.rem(to, NC)}
+
     barrier = pltpu.get_barrier_semaphore()
     for d in range(1, NZ):
         pl.semaphore_signal(barrier, inc=1, device_id={"z": lax.rem(z + d, NZ)}, device_id_type=pl.DeviceIdType.MESH)
     for d in range(1, NY):
         pl.semaphore_signal(barrier, inc=1, device_id={"y": lax.rem(y + d, NY)}, device_id_type=pl.DeviceIdType.MESH)
-    for d in range(1, NX):
-        pl.semaphore_signal(barrier, inc=1, device_id={"x": lax.rem(x + d, NX)}, device_id_type=pl.DeviceIdType.MESH)
-    pl.semaphore_signal(barrier, inc=1, device_id={"core": other}, device_id_type=pl.DeviceIdType.MESH)
-
+    for e in range(1, NX * NC):
+        pl.semaphore_signal(barrier, inc=1, device_id=group_peer(e), device_id_type=pl.DeviceIdType.MESH)
     own_x = pltpu.make_async_copy(
         x_hbm.at[:, pl.ds(pl.multiple_of(y * QUARTER, QUARTER), QUARTER)], rows(xq, y * RUN, RUN), local_sem
     )
@@ -100,13 +105,16 @@
     shrink_x[...] = jnp.exp(cum_x[RUN - 1 :, :] - cum_x)
     dg[...] = (dy_ref[...].astype(F32) * grow_x[...]).astype(BF16)
 
+    first_rows = lax.broadcasted_iota(jnp.int32, (16, STATES), 0) < 8
+
+    def two_terms(decay):
+        decay = jnp.broadcast_to(decay, (16, STATES))
+        high = decay.astype(BF16).astype(F32)
+        return jnp.where(first_rows, high, decay - high).astype(BF16)
+
     def scan_pack(states, sent):
         for k in range(HEADS):
             sent[k, :DEPTH, :] = states[k * DEPTH : (k + 1) * DEPTH].astype(BF16)
-            decay = jnp.exp(jnp.broadcast_to(cum[RUN - 1 :, k : k + 1], (16, STATES)))
-            high = decay.astype(BF16)
-            sent[k, DEPTH : DEPTH + 16, :] = high
-            sent[k, DEPTH + 16 :, :] = (decay - high.astype(F32)).astype(BF16)
 
     def scan_out(sent, got, base):
         for d in (4, 3, 5, 2, 6, 1, 7):
@@ -115,7 +123,9 @@
         got[pl.ds(z, 1)] = sent[pl.ds(z, 1)]
 
     scan_pack(dot(dg[...], c_ref[...], ((0,), (0,))), b1)
-    pl.semaphore_wait(barrier, NZ + NY + NX - 2)
+    for k in range(HEADS):
+        b1[k, DEPTH:, :] = two_terms(jnp.exp(cum[RUN - 1 :, k : k + 1]))
+    pl.semaphore_wait(barrier, NZ + NY + NX * NC - 3)
     scan_out(b1, r1, M_BACK)
 
     ring_z = (lax.rem(z + 1, NZ), lax.rem(z + NZ - 1, NZ))
@@ -170,24 +180,22 @@
                 arrived(x_piece(source, lax.rem(x + NX - e, NX)), M_XX + (d - 1) * 3 + e - 1, x=lax.rem(x + 1, NX))
             send(x_part(source, core), x_part(source, core), M_XS + d - 1, core=other)
 
-    def unpack(ref, k):
-        decay = ref[k, DEPTH : DEPTH + 16, :].astype(F32) + ref[k, DEPTH + 16 :, :].astype(F32)
-        return ref[k, :DEPTH, :].astype(F32), decay[:1, :]
-
-    def scan_rows(got, sent, got_y, base, order):
+    def unpack(ref, decays, k):
+        terms = decays[k, DEPTH:, :].astype(F32)
+        return ref[k, :DEPTH, :].astype(F32), terms[:1, :] + terms[8:9, :]
+
+    def scan_rows(got, sent, got_y, base, order, with_decay):
         for d in range(1, NZ):
             arrived(got.at[lax.rem(z + NZ - d, NZ)], base + d - 1, z=ring_z[0])
         carried, decays = jnp.zeros((DEPTH, STATES), F32), jnp.ones((1, STATES), F32)
         for k in order:
-            state, decay = unpack(got, k)
+            state, decay = unpack(got, r1, k)
             carried = decay * carried + state
             decays = decays * decay
-        decays = jnp.broadcast_to(decays, (16, STATES))
-        high = decays.astype(BF16)
         sent[:DEPTH, :] = carried.astype(BF16)
-        sent[DEPTH : DEPTH + 16, :] = high
-        sent[DEPTH + 16 :, :] = (decays - high.astype(F32)).astype(BF16)
-        for d in range(1, NY):
+        if with_decay:
+            sent[DEPTH:, :] = two_terms(decays)
+        for d in (2, 1, 3):
             to = lax.rem(y + d, NY)
             send(sent, got_y.at[y], base + 7 + d - 1, y=to)
         got_y[pl.ds(y, 1)] = sent[...][None]
@@ -197,14 +205,14 @@
             arrived(got_y.at[lax.rem(y + NY - d, NY)], base + 7 + d - 1, y=lax.rem(y + 1, NY))
         carried = jnp.zeros((DEPTH, STATES), F32)
         for k in reversed(range(NY)) if reverse else range(NY):
-            state, decay = unpack(got_y, k)
+            state, decay = unpack(got_y, r2, k)
             reached = (y < k) if reverse else (y > k)
             carried = jnp.where(reached, decay * carried + state, carried)
         for k in order:
             sent[k] = carried.astype(BF16)
-            state, decay = unpack(got, k)
+            state, decay = unpack(got, r1, k)
             carried = decay * carried + state
-        for d in range(1, NZ):
+        for d in (4, 3, 5, 2, 6, 1, 7):
             to = lax.rem(z + d, NZ)
             send(sent.at[to], got_z.at[z], base + 10 + d - 1, z=to)
         got_z[pl.ds(z, 1)] = sent[pl.ds(z, 1)]
@@ -233,16 +241,12 @@
             total = total + dot((decay * scores).astype(BF16), kept)
         gvi[:, columns] = total
 
-    within(0)
-    within(1)
+    for pair in range(HEADS // 2):
+        within(pair)
+    scan_rows(r1, b2, r2, M_BACK, down, True)
+    scan_back(r1, r2, b3, r3, M_BACK, down, True)
+    x_relay()
     w_step(1)
-    scan_rows(r1, b2, r2, M_BACK, down)
-    x_relay()
-    within(2)
-    within(3)
-    w_step(2)
-    scan_back(r1, r2, b3, r3, M_BACK, down, True)
-    w_step(3)
     scan_in(r3, M_BACK, gin)
 
     def g_part(ref, row):
@@ -254,37 +258,36 @@
         send(g_part(gq, y), g_part(gq, y), M_G + d - 1, y=lax.rem(y + d, NY))
     send(g_part(gq, y), g_part(gs, y), M_GS, core=other)
 
+    w_step(2)
+    w_step(3)
+    for d in (1, 3, 2):
+        source = lax.rem(y + NY - d, NY)
+        arrived(g_part(gq, source), M_G + d - 1, y=lax.rem(y + 1, NY))
+        send(g_part(gq, source), g_part(gs, source), M_GS + d, core=other)
     w_step(4)
     theirs = pl.multiple_of(other * SLICE, SLICE)
     mine = pl.multiple_of(core * SLICE, SLICE)
     send(wq.at[pl.ds(theirs, SLICE), :], ws, M_WS, core=other)
     x_collect()
     own_x.wait()
-    for d in (1, 3, 2):
-        source = lax.rem(y + NY - d, NY)
-        arrived(g_part(gq, source), M_G + d - 1, y=lax.rem(y + 1, NY))
-        send(g_part(gq, source), g_part(gs, source), M_GS + d, core=other)
-    for d in range(1, NY):
-        arrived(x_part(lax.rem(y + NY - d, NY), other), M_XS + d - 1, core=other)
 
     def gw_own(dest):
         columns = pl.ds(pl.multiple_of(dest * RUN, RUN), RUN)
         return dot(xq[:, columns], gq[...], ((0,), (0,)))
 
     def gw_step(t):
-        for way in (0, 1):
-            dest = lax.rem(z + 4 - t, NZ) if way == 0 else lax.rem(z + 4 + t, NZ)
-            own = gw_own(dest)
-            for half in (way, 1 - way):
-                if t == 0 and half != way:
-                    continue
-                part = own[half * HALF : (half + 1) * HALF]
-                index = way * 8 + t * 2 + half
-                if t > 1 or (t == 1 and half == way):
-                    arrived(gwr.at[way, t - 1, half], M_GW + index - 2, z=ring_z[way])
-                    part = part + gwr[way, t - 1, half].astype(F32)
-                gws[way, t, half] = part.astype(BF16)
-                send(gws.at[way, t, half], gwr.at[way, t, half], M_GW + index, z=ring_z[way])
+        dests = (lax.rem(z + 4 - t, NZ), lax.rem(z + 4 + t, NZ))
+        own = [gw_own(dest) for dest in dests]
+        for way, half in ((0, 0), (1, 1), (0, 1), (1, 0)):
+            if t == 0 and half != way:
+                continue
+            part = own[way][half * HALF : (half + 1) * HALF]
+            index = way * 8 + t * 2 + half
+            if t > 1 or (t == 1 and half == way):
+                arrived(gwr.at[way, t - 1, half], M_GW + index - 2, z=ring_z[way])
+                part = part + gwr[way, t - 1, half].astype(F32)
+            gws[way, t, half] = part.astype(BF16)
+            send(gws.at[way, t, half], gwr.at[way, t, half], M_GW + index, z=ring_z[way])
 
     def gw_end():
         own = gw_own(z)
@@ -295,21 +298,6 @@
                 part = part + gwr[way, 3, half].astype(F32)
             gw_ref[half * HALF : (half + 1) * HALF, :] = part
 
-    def four_step(t, axis, me, own, sent, got, base):
-        ends = []
-        for way in (0, 1):
-            dest = lax.rem(me + 3 - t, 4) if way == 0 else lax.rem(me + 1 + t, 4)
-            to = lax.rem(me + 1, 4) if way == 0 else lax.rem(me + 3, 4)
-            part = own(dest, way)
-            if t > 0:
-                arrived(got.at[way, t - 1], base + way * 3 + t - 1, **{axis: to})
-                part = part + got[way, t - 1].astype(F32)
-            if t < 3:
-                sent[way, t] = part.astype(BF16)
-                send(sent.at[way, t], got.at[way, t], base + way * 3 + t, **{axis: to})
-            ends.append(part)
-        return ends
-
     turn = lax.rem(x + NX - y, NX)
 
     def gi_rows(block, way, sub):
@@ -322,81 +310,93 @@
         )
 
     def chain(slot):
+        chain_step(slot, False)
+
+    def chain_start():
+        for i in range(8):
+            chain_step(i, True)
+
+    def chain_step(slot, start):
         for way in (0, 1):
             place = lax.rem(turn + 3, NX) if way == 0 else lax.rem(7 - turn, NX)
             to = lax.rem(x + 1, NX) if way == 0 else lax.rem(x + 3, NX)
-            i = slot - place
-
-            @pl.when((i >= 0) & (i < 8))
+            i = slot if start else slot - place
+
+            @pl.when((place == 0) if start else ((place > 0) & (i >= 0) & (i < 8)))
             def _(way=way, place=place, to=to, i=i):
-                block, sub = lax.rem(y + lax.div(i, 2), NY), lax.rem(i, 2)
+                block, sub = lax.rem(y + 1 + lax.div(i, 2), NY), lax.rem(i, 2)
                 index = M_C + way * 8 + i
                 own = gia[gi_rows(block, way, sub), :]
 
-                @pl.when(place == 0)
-                def _():
-                    gis[way, pl.ds(i, 1)] = own.astype(BF16)[None]
-
-                @pl.when(place > 0)
-                def _():
-                    arrived(gir.at[way, i], index, x=to)
-                    gis[way, pl.ds(i, 1)] = (own[None] + gir[way, pl.ds(i, 1)].astype(F32)).astype(BF16)
+                if start:
+                    gis[way, i] = own.astype(BF16)
+                    message(gis.at[way, i], gir.at[way, i], index, x=to).start()
+                    return
+                arrived(gir.at[way, i], index, x=to)
+                gis[way, pl.ds(i, 1)] = (own[None] + gir[way, pl.ds(i, 1)].astype(F32)).astype(BF16)
 
                 @pl.when(place < 3)
                 def _():
                     message(gis.at[way, i], gir.at[way, i], index, x=to).start()
 
-                @pl.when((place == 3) & (i < 2))
+                @pl.when((place == 3) & (i >= 6))
                 def _():
                     gi_fin[gi_rows(0, way, sub), :] = gis[way, pl.ds(i, 1)][0]
 
-                @pl.when((place == 3) & (i >= 2))
+                @pl.when((place == 3) & (i < 6))
                 def _():
                     message(
                         gis.at[way, i], gi_fin.at[gi_rows(0, way, sub), :], index, M_D + way * 2 + sub, y=block
                     ).start()
 
-    gw_step(0)
+    def product(start):
+        def one_run(k, _):
+            block = pl.ds(pl.multiple_of(k * RUN, RUN), RUN)
+            part = dot(xq[block, pl.ds(start, SLICE)], wq[pl.ds(start, SLICE), :])
+            acc[block, :] = part if start is mine else acc[block, :] + part
+            return 0
+
+        lax.fori_loop(0, NY, one_run, 0)
+
+    def v_send():
+        for d in (2, 1, 3):
+            to = lax.rem(y + d, NY)
+            vs[d - 1] = acc[pl.ds(pl.multiple_of(to * RUN, RUN), RUN), :].astype(BF16)
+            send(vs.at[d - 1], vr.at[d - 1], M_V + d - 1, y=to)
+
+    def v_end():
+        total = acc[pl.ds(pl.multiple_of(y * RUN, RUN), RUN), :]
+        for d in (1, 3, 2):
+            arrived(vr.at[d - 1], M_V + d - 1, y=lax.rem(y + 1, NY))
+            total = total + vr[d - 1].astype(F32)
+        vals[...] = total.astype(BF16)
+        xs[...] = (vals[...].astype(F32) * shrink_x[...]).astype(BF16)
+
+    product(mine)
     arrived(ws, M_WS, core=other)
     for d in range(NY):
         arrived(g_part(gs, lax.rem(y + NY - d, NY)), M_GS + d, core=other)
-    gi_product(0)
-    chain(0)
-    gi_product(1)
-    gi_product(2)
-    gi_product(3)
-
-    def product(k, _):
-        block = pl.ds(pl.multiple_of(k * RUN, RUN), RUN)
-        acc[block, :] = dot(xq[block, :], wq[...])
-        return 0
-
-    lax.fori_loop(0, NY, product, 0)
-
-    def v_own(dest, half):
-        return acc[pl.ds(pl.multiple_of(dest * RUN + half * HALF, HALF), HALF), :]
-
-    def v_step(t):
-        return four_step(t, "y", y, v_own, vs, vr, M_V)
-
-    v_step(0)
+    for d in range(NY):
+        gi_product(d)
+    chain_start()
+    for d in range(1, NY):
+        arrived(x_part(lax.rem(y + NY - d, NY), other), M_XS + d - 1, core=other)
+    product(theirs)
+    v_send()
+    gw_step(0)
     chain(1)
+    chain(2)
     gw_step(1)
-    chain(2)
-    v_step(1)
     chain(3)
-    v_step(2)
-    gw_step(2)
-    chain(4)
-    for half, part in enumerate(v_step(3)):
-        vals[half * HALF : (half + 1) * HALF, :] = part.astype(BF16)
-    xs[...] = (vals[...].astype(F32) * shrink_x[...]).astype(BF16)
+    v_end()
     scan_pack(dot(xs[...], b_ref[...], ((0,), (0,))), f1)
     scan_out(f1, p1, M_FORE)
+    chain(4)
+    gw_step(2)
+    scan_rows(p1, f2, p2, M_FORE, up, False)
     chain(5)
     gw_step(3)
     chain(6)
-    scan_rows(p1, f2, p2, M_FORE, up)
 
     mixed = jnp.zeros((RUN, RUN), F32)
     for pair in range(HEADS // 2):
@@ -408,31 +408,36 @@
     mixed = mixed.astype(BF16)
     grad_b = dot(mixed, c_ref[...]) + dot(xs[...], gin[...])
     grad_c = dot(mixed, b_ref[...], ((0,), (0,)))
+    scan_back(p1, p2, f3, p3, M_FORE, up, False)
     chain(7)
-    scan_back(p1, p2, f3, p3, M_FORE, up, False)
+    gw_end()
     chain(8)
-    gw_end()
-    chain(9)
     scan_in(p3, M_FORE, hin)
     grad_c = grad_c + dot(dg[...], hin[...])
 
-    sib_send[...] = jnp.where(core == 0, grad_c, grad_b)
-    send(sib_send, sib_recv, M_S, core=other)
-    arrived(sib_recv, M_S, core=other)
-    red[pl.ds(x, 1)] = (jnp.where(core == 0, grad_b, grad_c) + sib_recv[...]).astype(BF16)[None]
-    for d in range(1, NX):
-        send(red.at[x], red.at[x], M_S + d, x=lax.rem(x + d, NX))
+    for k in range(NX * NC):
+        share = slice(k * EIGHTH, (k + 1) * EIGHTH)
+        part_send[k, :EIGHTH, :] = grad_b[share].astype(BF16)
+        part_send[k, EIGHTH:, :] = grad_c[share].astype(BF16)
+    for e in range(1, NX * NC):
+        send(part_send.at[lax.rem(me + e, NX * NC)], part_recv.at[me], M_S + e - 1, **group_peer(e))
+    part_recv[pl.ds(me, 1)] = part_send[pl.ds(me, 1)]
+    chain(9)
+    for e in range(1, NX * NC):
+        arrived(part_recv.at[lax.rem(me + NX * NC - e, NX * NC)], M_S + e - 1, **group_peer(e))
+    total = part_recv[0].astype(F32)
+    for k in range(1, NX * NC):
+        total = total + part_recv[k].astype(F32)
+    sums[pl.ds(me, 1)] = total.astype(BF16)[None]
+    for e in range(1, NX * NC):
+        send(sums.at[me], sums.at[me], M_S + 7 + e - 1, **group_peer(e))
     chain(10)
-    for d in range(1, NX):
-        arrived(red.at[lax.rem(x + NX - d, NX)], M_S + d, x=lax.rem(x + 1, NX))
-    total = red[0].astype(F32)
-    for k in range(1, NX):
-        total = total + red[k].astype(F32)
-    tot_send[...] = total
-    send(tot_send, tot_recv, M_S + 4, core=other)
-    arrived(tot_recv, M_S + 4, core=other)
-    gb_ref[...] = jnp.where(core == 0, tot_send[...], tot_recv[...])
-    gc_ref[...] = jnp.where(core == 0, tot_recv[...], tot_send[...])
+    for e in range(1, NX * NC):
+        arrived(sums.at[lax.rem(me + NX * NC - e, NX * NC)], M_S + 7 + e - 1, **group_peer(e))
+    for k in range(NX * NC):
+        share = slice(k * EIGHTH, (k + 1) * EIGHTH)
+        gb_ref[share, :] = sums[k, :EIGHTH, :].astype(F32)
+        gc_ref[share, :] = sums[k, EIGHTH:, :].astype(F32)
 
     @pl.when(x != y)
     def _():
@@ -444,7 +449,7 @@
     for way in (0, 1):
         for i in range(8):
             sent = message(gis.at[way, i], gir.at[way, i], M_C + way * 8 + i, x=lax.rem(x + 1, NX))
-            if i >= 2:
+            if i < 6:
                 sent.wait_send()
             else:
                 pl.when(x != y)(sent.wait_send)
@@ -464,12 +469,14 @@
     def pair(count, *rest):
         return [pltpu.VMEM((count, *rest), BF16)] * 2
 
-    scan = [
-        *pair(HEADS, PACK, STATES),
-        pltpu.VMEM((PACK, STATES), BF16),
-        pltpu.VMEM((NY, PACK, STATES), BF16),
-        *pair(HEADS, DEPTH, STATES),
-    ]
+    def scan(rows):
+        return [
+            *pair(HEADS, rows, STATES),
+            pltpu.VMEM((rows, STATES), BF16),
+            pltpu.VMEM((NY, rows, STATES), BF16),
+            *pair(HEADS, DEPTH, STATES),
+        ]
+
     results = pl.pallas_call(
         kernel,
         out_shape=(
@@ -495,19 +502,16 @@
             pltpu.VMEM((RUN, COLS), BF16),
             pltpu.VMEM((HEADS * DEPTH, STATES), BF16),
             pltpu.VMEM((HEADS * DEPTH, STATES), BF16),
-            *scan,
-            *scan,
+            *scan(PACK),
+            *scan(DEPTH),
             pltpu.VMEM((NY * RUN, COLS), F32),
             pltpu.VMEM((NY * RUN, SLICE), F32),
-            *pair(2, 3, HALF, COLS),
+            *pair(3, RUN, COLS),
             *pair(2, 4, 2, HALF, COLS),
             *pair(2, 8, PIECE, SLICE),
             pltpu.VMEM((RUN, SLICE), BF16),
-            pltpu.VMEM((RUN, STATES), F32),
-            pltpu.VMEM((RUN, STATES), F32),
-            pltpu.VMEM((NX, RUN, STATES), BF16),
-            pltpu.VMEM((RUN, STATES), F32),
-            pltpu.VMEM((RUN, STATES), F32),
+            *pair(NX * NC, 2 * EIGHTH, STATES),
+            pltpu.VMEM((NX * NC, 2 * EIGHTH, STATES), BF16),
             pltpu.SemaphoreType.DMA((MESSAGES,)),
             pltpu.SemaphoreType.DMA((MESSAGES,)),
             pltpu.SemaphoreType.DMA,

time: 113 us -> 101 us (0.89); the launches traced: 113 us -> 99.6 us
  Pallas kernels: 113 us -> 99 us
    pallas_call x1, Pallas kernels: 110 us -> 96.6 us  [per_device(): pl.pallas_call(kernel, out_shape=(jax.ShapeDtypeStruct((RUN, SLICE), BF16...]
where the time goes in v4:
time: 101 us; the launch traced here: 99.6 us
  Pallas kernels  99 us (98%)
    pallas_call x1, Pallas kernels, per_device(): pl.pallas_call(kernel, out_shape=(jax.ShapeDtypeStruct((RUN, SLICE), BF16...  96.6 us
    pallas_call x1, Pallas kernels, per_device(): pl.pallas_call(hand_over, out_shape=tuple((jax.ShapeDtypeStruct(r.shape,...  2.34 us

profile of v4, /device:TPU:1, one launch (start us, length us, event | category | flops | bytes accessed | tf_op | source)
XLA Modules:
  0.0 99.6 jit_solution(16086486592526804532)
XLA Ops:
  0.6 96.6 %ssd_backward.1 = (bf16[256,1024]{1,0:T(8,128)(2,1)}, f32[256,512]{1,0:T(8,128)}, f32[256,128]{1,0:T(8,128)}, f32[256,128]{1,0:T(8,128)}) custom-call(bf16[256,8192]{1,0:T(8,128)(2,1)} %x_hbm.1, bf16[256,512]{1,0:T(8,128)(2,1)} %w_ref.1, f32[8,256]{1,0:T(8,128)} %bitcast.1, bf16[256,128]{1,0:T(8,128)(2,1)} %b_ref.1, bf16[256,128]{1,0:T(8,128)(2,1)} %c_ref.1, ...), custom_call_target="tpu_custom_call" | custom-call | tf_op jit(solution)/shard_map/ssd_backward/pallas_call | solution.py:480
  97.2 2.3 %hand_over.1 = (bf16[256,1024]{1,0:T(8,128)(2,1)}, f32[256,512]{1,0:T(8,128)}, f32[256,128]{1,0:T(8,128)}, f32[256,128]{1,0:T(8,128)}) custom-call(bf16[256,1024]{1,0:T(8,128)(2,1)} %get-tuple-element.8.refs_0_, f32[256,512]{1,0:T(8,128)} %get-tuple-element.9.refs_1_, f32[256,128]{1,0:T(8,128)} %get-tuple-element.10.refs_2_, ...), custom_call_target="tpu_custom_call" | custom-call | tf_op jit(solution)/shard_map/hand_over/pallas_call | solution.py:524

commit v5 on v4

--- a/solution.py
+++ b/solution.py
@@ -32,7 +32,7 @@
 M_G = M_FORE + 17
 M_GS = M_G + 3
 M_V = M_GS + 4
-M_GW = M_V + 3
+M_GW = M_V + 6
 M_C = M_GW + 16
 M_D = M_C + 16
 M_S = M_D + 4
@@ -358,18 +358,33 @@
 
         lax.fori_loop(0, NY, one_run, 0)
 
+    near = (lax.rem(y + 1, NY), lax.rem(y + 3, NY))
+
+    def v_part(run, half):
+        return acc[pl.ds(pl.multiple_of(run * RUN + half * HALF, HALF), HALF), :]
+
+    def v_out(part, way, k):
+        vs[way, k] = part.astype(BF16)
+        send(vs.at[way, k], vr.at[way, k], M_V + way * 3 + k, y=near[way])
+
+    def v_in(way, k):
+        arrived(vr.at[way, k], M_V + way * 3 + k, y=near[way])
+        return vr[way, k].astype(F32)
+
     def v_send():
-        for d in (2, 1, 3):
-            to = lax.rem(y + d, NY)
-            vs[d - 1] = acc[pl.ds(pl.multiple_of(to * RUN, RUN), RUN), :].astype(BF16)
-            send(vs.at[d - 1], vr.at[d - 1], M_V + d - 1, y=to)
+        for way in (0, 1):
+            v_out(v_part(lax.rem(y + 2, NY), way), way, 0)
+        for way in (0, 1):
+            v_out(v_part(near[way], 1 - way), way, 1)
+
+    def v_relay():
+        for way in (0, 1):
+            v_out(v_part(near[way], way) + v_in(way, 0), way, 2)
 
     def v_end():
-        total = acc[pl.ds(pl.multiple_of(y * RUN, RUN), RUN), :]
-        for d in (1, 3, 2):
-            arrived(vr.at[d - 1], M_V + d - 1, y=lax.rem(y + 1, NY))
-            total = total + vr[d - 1].astype(F32)
-        vals[...] = total.astype(BF16)
+        for half in (0, 1):
+            total = v_part(y, half) + v_in(1 - half, 1) + v_in(half, 2)
+            vals[half * HALF : (half + 1) * HALF, :] = total.astype(BF16)
         xs[...] = (vals[...].astype(F32) * shrink_x[...]).astype(BF16)
 
     product(mine)
@@ -384,18 +399,18 @@
     product(theirs)
     v_send()
     gw_step(0)
+    v_relay()
     chain(1)
+    gw_step(1)
     chain(2)
-    gw_step(1)
-    chain(3)
     v_end()
     scan_pack(dot(xs[...], b_ref[...], ((0,), (0,))), f1)
     scan_out(f1, p1, M_FORE)
+    chain(3)
     chain(4)
     gw_step(2)
     scan_rows(p1, f2, p2, M_FORE, up, False)
     chain(5)
-    gw_step(3)
     chain(6)
 
     mixed = jnp.zeros((RUN, RUN), F32)
@@ -409,8 +424,8 @@
     grad_b = dot(mixed, c_ref[...]) + dot(xs[...], gin[...])
     grad_c = dot(mixed, b_ref[...], ((0,), (0,)))
     scan_back(p1, p2, f3, p3, M_FORE, up, False)
+    gw_step(3)
     chain(7)
-    gw_end()
     chain(8)
     scan_in(p3, M_FORE, hin)
     grad_c = grad_c + dot(dg[...], hin[...])
@@ -423,6 +438,7 @@
         send(part_send.at[lax.rem(me + e, NX * NC)], part_recv.at[me], M_S + e - 1, **group_peer(e))
     part_recv[pl.ds(me, 1)] = part_send[pl.ds(me, 1)]
     chain(9)
+    gw_end()
     for e in range(1, NX * NC):
         arrived(part_recv.at[lax.rem(me + NX * NC - e, NX * NC)], M_S + e - 1, **group_peer(e))
     total = part_recv[0].astype(F32)
@@ -506,7 +522,7 @@
             *scan(DEPTH),
             pltpu.VMEM((NY * RUN, COLS), F32),
             pltpu.VMEM((NY * RUN, SLICE), F32),
-            *pair(3, RUN, COLS),
+            *pair(2, 3, HALF, COLS),
             *pair(2, 4, 2, HALF, COLS),
             *pair(2, 8, PIECE, SLICE),
             pltpu.VMEM((RUN, SLICE), BF16),

time: 101 us -> 98.7 us (0.977); the launches traced: 99.6 us -> 98.6 us
  Pallas kernels: 99 us -> 97.9 us
    pallas_call x1, Pallas kernels: 96.6 us -> 95.6 us  [per_device(): pl.pallas_call(kernel, out_shape=(jax.ShapeDtypeStruct((RUN, SLICE), BF16...]
where the time goes in v5:
time: 98.7 us; the launch traced here: 98.6 us
  Pallas kernels  97.9 us (99%)
    pallas_call x1, Pallas kernels, per_device(): pl.pallas_call(kernel, out_shape=(jax.ShapeDtypeStruct((RUN, SLICE), BF16...  95.6 us
    pallas_call x1, Pallas kernels, per_device(): pl.pallas_call(hand_over, out_shape=tuple((jax.ShapeDtypeStruct(r.shape,...  2.34 us

profile of v5, /device:TPU:1, one launch (start us, length us, event | category | flops | bytes accessed | tf_op | source)
XLA Modules:
  0.0 98.6 jit_solution(10103730132276593530)
XLA Ops:
  0.6 95.6 %ssd_backward.1 = (bf16[256,1024]{1,0:T(8,128)(2,1)}, f32[256,512]{1,0:T(8,128)}, f32[256,128]{1,0:T(8,128)}, f32[256,128]{1,0:T(8,128)}) custom-call(bf16[256,8192]{1,0:T(8,128)(2,1)} %x_hbm.1, bf16[256,512]{1,0:T(8,128)(2,1)} %w_ref.1, f32[8,256]{1,0:T(8,128)} %bitcast.1, bf16[256,128]{1,0:T(8,128)(2,1)} %b_ref.1, bf16[256,128]{1,0:T(8,128)(2,1)} %c_ref.1, ...), custom_call_target="tpu_custom_call" | custom-call | tf_op jit(solution)/shard_map/ssd_backward/pallas_call | solution.py:496
  96.2 2.3 %hand_over.1 = (bf16[256,1024]{1,0:T(8,128)(2,1)}, f32[256,512]{1,0:T(8,128)}, f32[256,128]{1,0:T(8,128)}, f32[256,128]{1,0:T(8,128)}) custom-call(bf16[256,1024]{1,0:T(8,128)(2,1)} %get-tuple-element.8.refs_0_, f32[256,512]{1,0:T(8,128)} %get-tuple-element.9.refs_1_, f32[256,128]{1,0:T(8,128)} %get-tuple-element.10.refs_2_, ...), custom_call_target="tpu_custom_call" | custom-call | tf_op jit(solution)/shard_map/hand_over/pallas_call | solution.py:540

commit v6 on v5

--- a/solution.py
+++ b/solution.py
@@ -244,8 +244,8 @@
     for pair in range(HEADS // 2):
         within(pair)
     scan_rows(r1, b2, r2, M_BACK, down, True)
+    x_relay()
     scan_back(r1, r2, b3, r3, M_BACK, down, True)
-    x_relay()
     w_step(1)
     scan_in(r3, M_BACK, gin)
 

time: 98.7 us -> 98.7 us (level)
  no operation moved by 1% of the time
where the time goes in v6:
time: 98.7 us; the launch traced here: 98.6 us
  Pallas kernels  97.9 us (99%)
    pallas_call x1, Pallas kernels, per_device(): pl.pallas_call(kernel, out_shape=(jax.ShapeDtypeStruct((RUN, SLICE), BF16...  95.6 us
    pallas_call x1, Pallas kernels, per_device(): pl.pallas_call(hand_over, out_shape=tuple((jax.ShapeDtypeStruct(r.shape,...  2.34 us

profile of v6, /device:TPU:1, one launch (start us, length us, event | category | flops | bytes accessed | tf_op | source)
XLA Modules:
  0.0 98.6 jit_solution(6314957231523014564)
XLA Ops:
  0.6 95.6 %ssd_backward.1 = (bf16[256,1024]{1,0:T(8,128)(2,1)}, f32[256,512]{1,0:T(8,128)}, f32[256,128]{1,0:T(8,128)}, f32[256,128]{1,0:T(8,128)}) custom-call(bf16[256,8192]{1,0:T(8,128)(2,1)} %x_hbm.1, bf16[256,512]{1,0:T(8,128)(2,1)} %w_ref.1, f32[8,256]{1,0:T(8,128)} %bitcast.1, bf16[256,128]{1,0:T(8,128)(2,1)} %b_ref.1, bf16[256,128]{1,0:T(8,128)(2,1)} %c_ref.1, ...), custom_call_target="tpu_custom_call" | custom-call | tf_op jit(solution)/shard_map/ssd_backward/pallas_call | solution.py:496
  96.2 2.3 %hand_over.1 = (bf16[256,1024]{1,0:T(8,128)(2,1)}, f32[256,512]{1,0:T(8,128)}, f32[256,128]{1,0:T(8,128)}, f32[256,128]{1,0:T(8,128)}) custom-call(bf16[256,1024]{1,0:T(8,128)(2,1)} %get-tuple-element.8.refs_0_, f32[256,512]{1,0:T(8,128)} %get-tuple-element.9.refs_1_, f32[256,128]{1,0:T(8,128)} %get-tuple-element.10.refs_2_, ...), custom_call_target="tpu_custom_call" | custom-call | tf_op jit(solution)/shard_map/hand_over/pallas_call | solution.py:540
